TPU v7x, 32 devices: a whole 2x2x4 slice. The times are simulated.
32 devices in a mesh: shot: 8 (over z, y), xline: 4 (over x, core).
Axes of the slice: x: 2, y: 2, z: 4, core: 2. Of those that a mesh axis runs over, the one named last changes fastest.
Arguments:
- records: bfloat16 [4, 16, 256, 2048], P('xline', 'shot'), may hold values from -1.796875 to 1.796875
- targets: bfloat16 [2048, 32, 256], P('xline', 'shot'), may hold values from -1.796875 to 1.796875
- aperture: int32 [32, 4, 16], P('shot', 'xline'), may hold values from 0 to 255
Outputs:
- multiples: bfloat16 [2048, 32, 256], P('xline', 'shot')
Inputs may be any that keep to these rules, and one draw needn't show every extreme that they name: An aperture entry is the receiver of the output shot at which the contributing source lies.
All inputs are finite; a program needn't handle non-finite values.
Results may differ from a plain program's by a relative error of at most 0.0071.
Values may be sent and summed in bfloat16 or wider, within the bound.
A program may use at most 128 MiB of HBM per device.

v0:
```python
import math

import jax
import jax.numpy as jnp
from jax import lax
from jax.sharding import PartitionSpec as P

NT = 2048
NF = 256


def forward_table():
    times_col = jnp.arange(NT, dtype=jnp.int32)[:, None]
    freq_row = jnp.arange(1, NF + 1, dtype=jnp.int32)[None, :]
    angles = (times_col * freq_row % NT).astype(jnp.float32) * (2.0 * math.pi / NT)
    normalizing_scale = 1.0 / math.sqrt(NT)
    return jnp.concatenate(
        [jnp.cos(angles) * normalizing_scale, -jnp.sin(angles) * normalizing_scale], axis=1
    ).astype(jnp.bfloat16)


def inverse_table():
    times_col = jnp.arange(NT, dtype=jnp.int32)[:, None]
    freq_row = jnp.arange(1, NF + 1, dtype=jnp.int32)[None, :]
    angles = (times_col * freq_row % NT).astype(jnp.float32) * (2.0 * math.pi / NT)
    normalizing_scale = 2.0 / math.sqrt(NT)
    stacked = jnp.stack(
        [jnp.cos(angles) * normalizing_scale, -jnp.sin(angles) * normalizing_scale], axis=2
    )
    return stacked.reshape(NT, 2 * NF)


def complex_mixing(real_part, imag_part):
    upper = jnp.stack([real_part, -imag_part], axis=1)
    lower = jnp.stack([imag_part, real_part], axis=1)
    return jnp.stack([upper, lower], axis=0)


def on_device(records, targets, aperture):
    forward_fourier = forward_table()
    shots_here = targets.shape[1]
    receivers = targets.shape[2]
    gathered = lax.all_gather(targets, "xline", axis=0, tiled=True)
    desired_spectra = jnp.einsum(
        "tsr,tp->srp", gathered, forward_fourier, preferred_element_type=jnp.float32
    ).astype(jnp.bfloat16)
    held = records.shape[1]
    trace_spectra = jnp.einsum(
        "hwn,ne->hew", records[0], forward_fourier, preferred_element_type=jnp.float32
    )
    trace_spectra = trace_spectra.astype(jnp.bfloat16).reshape(held, 2, NF, receivers)
    selects = aperture[:, 0, :]
    receiver_ids = jnp.arange(receivers, dtype=jnp.int32)
    onehot = (selects[:, :, None] == receiver_ids).astype(jnp.bfloat16)
    picked = jnp.einsum(
        "scr,srp->scp", onehot, desired_spectra, preferred_element_type=jnp.float32
    ).astype(jnp.bfloat16)
    mixing = complex_mixing(picked[:, :, :NF], picked[:, :, NF:])
    running = jnp.einsum(
        "qspcf,cpfr->fqsr",
        mixing,
        lax.all_gather(trace_spectra, "shot", axis=0, tiled=True),
        preferred_element_type=jnp.float32,
    )
    inverse_fourier = inverse_table()
    flat_traces = running.reshape(2 * NF, shots_here * receivers)
    time_rows = NT // lax.axis_size("xline")
    summed = lax.psum(flat_traces, "xline")
    inverse_rows = lax.dynamic_slice_in_dim(
        inverse_fourier, lax.axis_index("xline") * time_rows, time_rows, 0
    )
    local_part = jnp.dot(
        inverse_rows, summed, precision=lax.Precision.HIGHEST, preferred_element_type=jnp.float32
    )
    return local_part.reshape(time_rows, shots_here, receivers).astype(jnp.bfloat16)


def solution(mesh):
    in_specs = (P("xline", "shot", None, None), P("xline", "shot", None), P("shot", "xline", None))
    out_specs = P("xline", "shot", None)
    return jax.shard_map(
        on_device, mesh=mesh, in_specs=in_specs, out_specs=out_specs, check_vma=False
    )
```

profile of v0, /device:TPU:0, one launch (start us, length us, event | category | flops | bytes accessed | tf_op | source)
XLA Modules:
  0.0 191.9 jit_solution(8781376290301886159)
XLA Ops:
  6.5 0.0 copy-start
  6.5 0.0 all-gather.3.cloned.1.call-start
  6.5 0.7 all-gather.3.cloned.1.call-update
  7.3 0.0 all-gather.5.cloned.1.call-start
  7.3 9.1 %multiply_convert_fusion.1 = (bf16[2048,256]{0,1:T(8,128)(2,1)S(1)}, bf16[2048,256]{0,1:T(8,128)(2,1)S(1)}) fusion(s32[256]{0:T(256)S(1)} %iota_add_fusion), kind=kLoop, calls=%fused_computation.21 | loop fusion | flops 9961472 | bytes 2098176 | tf_op jit(solution)/shard_map/convert
  16.4 0.0 copy-start.1
  16.4 0.0 copy-done
  16.4 0.0 copy-start.2
  16.4 2.1 %fusion.24 = bf16[512,2,256]{2,0,1:T(8,128)(2,1)} fusion(bf16[1,2,256,2048]{3,2,1,0:T(8,128)(2,1)S(1)} %copy-done, bf16[2048,256]{0,1:T(8,128)(2,1)S(1)} %get-tuple-element.13, bf16[2048,256]{0,1:T(8,128)(2,1)S(1)} %get-tuple-element.12), kind=kOutput, calls=%fused_computation.33 | convolution fusion | flops 1078198272 | bytes 4718592 | tf_op jit(solution)/shard_map/hwn,ne->hew/dot_general | solution.py:48
  18.6 0.0 copy-done.1
  18.6 0.0 all-gather.5.cloned.1.call-update
  18.6 0.0 all-reduce.2.cloned.1.call-start
  18.6 27.5 %all-gather.3.cloned.1.call-done = bf16[2048,4,256]{2,1,0:T(4,128)(2,1)} async-done(((bf16[512,4,256]{2,1,0:T(4,128)(2,1)}), bf16[2048,4,256]{2,1,0:T(4,128)(2,1)}) %all-gather.3.cloned.1.call-update) | async-done | bytes 4194320 | tf_op jit(solution)/shard_map/all_gather | solution.py:43
  46.2 0.0 copy-done.2
  46.2 5.0 %fusion.30 = bf16[4,16,512]{2,1,0:T(8,128)(2,1)S(1)} fusion(bf16[2048,4,256]{2,1,0:T(4,128)(2,1)} %all-gather.3.cloned.1.call-done, bf16[2048,256]{0,1:T(8,128)(2,1)} %copy-done.1, bf16[2048,256]{0,1:T(8,128)(2,1)S(1)} %get-tuple-element.12, s32[4,16]{1,0:T(4,128)S(1)} %bitcast.49), kind=kOutput, calls=%fused_computation.35 | convolution fusion | flops 2169028608 | bytes 6357248 | tf_op jit(solution)/shard_map/scr,srp->scp/dot_general | solution.py:55
  51.3 1.1 copy.15
  52.4 68.8 %all-gather.5.cloned.1.call-done = bf16[16,2,256,256]{3,2,1,0:T(8,128)(2,1)} async-done(((bf16[2,2,256,256]{3,2,1,0:T(8,128)(2,1)}), bf16[16,2,256,256]{3,2,1,0:T(8,128)(2,1)}) %all-gather.5.cloned.1.call-update) | async-done | bytes 4194320 | tf_op jit(solution)/shard_map/all_gather | solution.py:62
  121.2 5.3 %fusion = f32[256,2,4,256,1]{3,2,4,1,0:T(4,128)S(1)} fusion(bf16[2,4,2,16,256]{3,1,2,0,4:T(4,128)(2,1)S(1)} %copy.15, bf16[16,2,256,256,1]{3,2,1,0,4:T(8,128)(2,1)} %bitcast.47), kind=kOutput, calls=%fused_computation.1 | convolution fusion | flops 33554432 | bytes 6422528 | tf_op jit(solution)/shard_map/qspcf,cpfr->fqsr/dot_general | solution.py:59
  126.5 1.8 copy.22
  128.3 0.0 all-reduce.2.cloned.1.call-update
  128.3 8.5 %cosine_multiply_fusion = (f32[2048,256,1]{1,0,2:T(8,128)S(1)}, f32[2048,256,1]{1,0,2:T(8,128)S(1)}) fusion(s32[256]{0:T(256)S(1)} %iota_add_fusion), kind=kLoop, calls=%fused_computation.25 | loop fusion | flops 8912896 | bytes 4195328 | tf_op jit(solution)/shard_map/mul | solution.py:28
  136.9 2.2 %pad_maximum_fusion = f32[2048,256,2]{1,0,2:T(8,128)} fusion(f32[2048,256,1]{1,0,2:T(8,128)S(1)} %get-tuple-element.11, f32[2048,256,1]{1,0,2:T(8,128)S(1)} %get-tuple-element.10), kind=kLoop, calls=%fused_computation | loop fusion | flops 1048576 | bytes 8388608 | tf_op jit(solution)/shard_map/stack | solution.py:27
  139.1 7.4 %copy.12 = f32[2048,256,2]{0,2,1:T(2,128)} copy(f32[2048,256,2]{1,0,2:T(8,128)} %pad_maximum_fusion) | data formatting | bytes 8388608 | tf_op jit(solution)/shard_map/stack | solution.py:27
  146.5 6.1 %reshape.122 = f32[2048,512]{0,1:T(8,128)} reshape(f32[2048,256,2]{0,2,1:T(2,128)} %copy.12) | data formatting | bytes 8388608 | tf_op jit(solution)/shard_map/reshape | solution.py:30
  152.6 25.8 %all-reduce.2.cloned.1.call-done = f32[512,1024]{1,0:T(8,128)} async-done(((f32[512,1024]{1,0:T(8,128)}), f32[512,1024]{1,0:T(8,128)}) %all-reduce.2.cloned.1.call-update) | async-done | bytes 2097168 | tf_op jit(solution)/shard_map/psum | solution.py:68
  178.4 5.4 %convolution_convert_fusion = bf16[512,1024]{1,0:T(8,128)(2,1)S(1)} fusion(f32[512,1024]{1,0:T(8,128)} %all-reduce.2.cloned.1.call-done, f32[2048,512]{0,1:T(8,128)} %reshape.122, s32[]{:T(128)S(6)} %select_n.30), kind=kOutput, calls=%fused_computation.30 | convolution fusion | flops 3221749760 | bytes 4194308 | tf_op jit(solution)/shard_map/dot_general | solution.py:72
  183.8 1.6 convert_element_type.52
  (4 shorter events, 0.1 us)
Async XLA Ops:
  6.5 9.9 %copy-start = (bf16[1,2,256,2048]{3,2,1,0:T(8,128)(2,1)S(1)}, bf16[1,2,256,2048]{3,2,1,0:T(8,128)(2,1)}, u32[]{:S(2)}) copy-start(bf16[1,2,256,2048]{3,2,1,0:T(8,128)(2,1)} %param.3) | copy-start | bytes 6291460
  6.5 39.6 %all-gather.3.cloned.1.call-start = ((), (), s32[]{:S(2)}) async-start(), calls=%async_computation | async-start | bytes 5242880 | tf_op jit(solution)/shard_map/all_gather | solution.py:43
  7.3 113.9 %all-gather.5.cloned.1.call-start = ((), (), s32[]{:S(2)}) async-start(), calls=%async_computation.1 | async-start | bytes 4718592 | tf_op jit(solution)/shard_map/all_gather | solution.py:62
  16.4 2.2 %copy-start.1 = (bf16[2048,256]{0,1:T(8,128)(2,1)}, bf16[2048,256]{0,1:T(8,128)(2,1)S(1)}, u32[]{:S(2)}) copy-start(bf16[2048,256]{0,1:T(8,128)(2,1)S(1)} %get-tuple-element.13) | copy-start | bytes 3145732
  16.4 29.8 %copy-start.2 = (s32[4,1,16]{2,1,0:T(1,128)S(1)}, s32[4,1,16]{2,1,0:T(1,128)}, u32[]{:S(2)}) copy-start(s32[4,1,16]{2,1,0:T(1,128)} %param.5) | copy-start | bytes 772
  18.6 159.8 %all-reduce.2.cloned.1.call-start = ((), (), s32[]{:S(2)}) async-start(), calls=%async_computation.2 | async-start | bytes 4194304 | tf_op jit(solution)/shard_map/psum | solution.py:68
Sparse Core Ops, SparseCore 0:
  8.9 37.2 all-gather.2
  48.3 72.8 all-gather.4
  128.4 49.9 all-reduce.1
where the time goes:
time: 192 us
  waiting for transfers between devices  123 us (64%)
  other arithmetic  19.9 us (10%)
  local copies, waits for them, and re-layouts  18 us (9%)
  matrix products  17.9 us (9%)
  between operations  13.2 us (7%)
    all_gather x1, waiting for transfers between devices, on_device(): lax.all_gather(trace_spectra, 'shot', axis=0, tiled=True)  68.8 us
    all_gather x1, waiting for transfers between devices, on_device(): gathered = lax.all_gather(targets, 'xline', axis=0, tiled=True)  27.5 us
    psum x1, waiting for transfers between devices, on_device(): summed = lax.psum(flat_traces, 'xline')  25.8 us
    another operation x1, other arithmetic  9.05 us
    mul x1, other arithmetic, inverse_table(): jnp.cos(angles) * normalizing_scale  8.53 us
    another operation x1, local copies, waits for them, and re-layouts, inverse_table(): jnp.stack([jnp.cos(angles) * normalizing_scale, -jnp.sin(angles) * normal...  7.43 us
    reshape x1, local copies, waits for them, and re-layouts, inverse_table(): return stacked.reshape(NT, 2 * NF)  6.09 us
    dot_general x1, matrix products, on_device(): jnp.dot(inverse_rows, summed, precision=lax.Precision.HIGHEST, preferred_...  5.4 us
  transfers between devices with their start and end apart: 3, of which 3 were waited for; matrix products, arithmetic and copies ran while one was open for 22% of the time, Pallas kernels for 0%

commit v1 on v0

v1 whole, which is shorter than its diff:
```python
import math

import jax
import jax.numpy as jnp
from jax import lax
from jax.sharding import PartitionSpec as P

NT = 2048
NF = 256
LOW = 32


def fourier_table(bins):
    blocks = NF // bins
    freq = jnp.arange(1, NF + 1, dtype=jnp.int32).reshape(blocks, 1, bins)
    freq = jnp.broadcast_to(freq, (blocks, 2, bins)).reshape(1, 2 * NF)
    is_imag = jnp.arange(2, dtype=jnp.int32).reshape(1, 2, 1)
    is_imag = jnp.broadcast_to(is_imag, (blocks, 2, bins)).reshape(1, 2 * NF) == 1

    def trig(times):
        angles = (times[:, None] * freq % NT).astype(jnp.float32) * (2.0 * math.pi / NT)
        return jnp.cos(angles), jnp.sin(angles)

    cos_hi, sin_hi = trig(jnp.arange(NT // LOW, dtype=jnp.int32) * LOW)
    cos_lo, sin_lo = trig(jnp.arange(LOW, dtype=jnp.int32))
    scale = 1.0 / math.sqrt(NT)
    first = jnp.where(is_imag, -sin_hi, cos_hi) * scale
    second = jnp.where(is_imag, -cos_hi, -sin_hi) * scale
    first, second, cos_lo, sin_lo = lax.optimization_barrier((first, second, cos_lo, sin_lo))
    table = first[:, None] * cos_lo[None] + second[:, None] * sin_lo[None]
    return table.reshape(NT, 2 * NF).astype(jnp.bfloat16)


def on_device(records, targets, aperture):
    f32, bf16 = jnp.float32, jnp.bfloat16
    lines = lax.axis_size("xline")
    columns = lax.axis_size("shot")
    devices = lines * columns
    bins = NF // devices
    time_rows, shots, receivers = targets.shape
    held = records.shape[1]
    gathers = aperture.shape[2]
    table = fourier_table(bins)

    apertures = lax.all_to_all(
        jnp.broadcast_to(aperture.reshape(1, shots, gathers), (lines, shots, gathers)),
        "xline", 0, 0, tiled=True,
    )
    receiver_ids = jnp.arange(receivers, dtype=jnp.int32)
    chosen = apertures.transpose(1, 0, 2).reshape(shots, lines * gathers)
    onehot = (chosen[:, :, None] == receiver_ids).astype(bf16)
    traces = jnp.einsum("skr,tsr->skt", onehot, targets, preferred_element_type=f32).astype(bf16)
    traces = traces.reshape(shots, lines, gathers, time_rows).transpose(1, 0, 2, 3)
    traces = lax.all_to_all(
        traces.reshape(lines, shots * gathers, time_rows), "xline", 0, 0, tiled=True
    )
    traces = traces.transpose(1, 0, 2).reshape(shots * gathers, NT)
    picked = jnp.einsum("tp,kt->pk", table, traces, preferred_element_type=f32).astype(bf16)

    spectra = jnp.einsum(
        "tp,kt->pk", table, records.reshape(held * receivers, NT), preferred_element_type=f32
    ).astype(bf16)

    width = held * receivers
    both = jnp.concatenate([spectra, picked], axis=1).reshape(devices, 2 * bins, -1)
    both = lax.all_to_all(both, ("xline", "shot"), 0, 0, tiled=True)
    spectra = both[:, :, :width].reshape(devices, 2 * bins, held, receivers)
    picked = both[:, :, width:].reshape(lines, columns, 2, bins, shots, columns, held)

    real, imag = picked[:, :, 0], picked[:, :, 1]
    mixing = jnp.stack(
        [jnp.stack([real, -imag], 0), jnp.stack([imag, real], 0)], 0
    )
    eye = jnp.eye(bins, dtype=bf16)
    mixing = jnp.einsum("xqldfsch,fg->dxfslcqgh", mixing, eye).astype(bf16)
    mixing = mixing.reshape(columns * 2 * bins * shots, devices, 2 * bins, held)
    running = jnp.einsum(
        "mvph,vphr->mr", mixing, spectra, preferred_element_type=f32
    ).astype(bf16)
    running = running.reshape(columns, 2 * bins * shots, receivers)
    running = lax.all_to_all(running, "shot", 0, 0, tiled=True)
    running = lax.all_gather(running, "xline", axis=0, tiled=True)
    running = running.reshape(2 * NF, shots, receivers)

    rows = lax.dynamic_slice_in_dim(table, lax.axis_index("xline") * time_rows, time_rows, 0)
    out = jnp.einsum("tp,psr->tsr", rows * 2, running, preferred_element_type=f32)
    return out.astype(bf16)


def solution(mesh):
    in_specs = (P("xline", "shot", None, None), P("xline", "shot", None), P("shot", "xline", None))
    out_specs = P("xline", "shot", None)
    return jax.shard_map(
        on_device, mesh=mesh, in_specs=in_specs, out_specs=out_specs, check_vma=False
    )
```

time: 192 us -> 151 us (0.79)
  waiting for transfers between devices: 123 us -> 38.2 us
  local copies, waits for them, and re-layouts: 18 us -> 41.5 us
  starting transfers between devices: 0.08 us -> 13.1 us
  blocking collectives: 0 us -> 12.2 us
  matrix products: 17.9 us -> 13.6 us
  other arithmetic: 19.9 us -> 17.5 us
    all_gather x2 -> x1, waiting for transfers between devices: 96.3 us -> 15.5 us  [on_device(): running = lax.all_gather(running, 'xline', axis=0, tiled=True)]
    psum x1 -> x0, waiting for transfers between devices: 25.8 us -> none  [on_device(): summed = lax.psum(flat_traces, 'xline')]
    all_to_all x0 -> x3, waiting for transfers between devices: none -> 22.6 us  [the longest x1 19 us: on_device(): both = lax.all_to_all(both, ('xline', 'shot'), 0, 0, tiled=True)]
    reshape x1 -> x6, local copies, waits for them, and re-layouts: 6.09 us -> 23.4 us  [the longest x1 20 us: on_device(): mixing = mixing.reshape(columns * 2 * bins * shots, devices, 2 * bins, held)]
    all_to_all x0 -> x3, starting transfers between devices: none -> 13 us  [the longest x1 5.39 us: on_device(): both = lax.all_to_all(both, ('xline', 'shot'), 0, 0, tiled=True)]
    all_to_all x0 -> x1, blocking collectives: none -> 12.2 us  [on_device(): running = lax.all_to_all(running, 'shot', 0, 0, tiled=True)]
    transpose x0 -> x1, other arithmetic: none -> 9.65 us  [on_device(): mixing = jnp.einsum('xqldfsch,fg->dxfslcqgh', mixing, eye).astype(bf16)]
    mul x1 -> x2, other arithmetic: 8.53 us -> 0.62 us  [the longest x1 0.62 us: fourier_table(): second = jnp.where(is_imag, -cos_hi, -sin_hi) * scale]
  transfers between devices with their start and end apart: 3 -> 4, of which waited for: 3 -> 4; matrix products, arithmetic and copies ran while one was open for 22% -> 4% of each run, Pallas kernels for 0% -> 0%
where the time goes in v1:
time: 151 us; the launch traced here: 150 us
  local copies, waits for them, and re-layouts  41.5 us (27%)
  waiting for transfers between devices  38.2 us (25%)
  other arithmetic  17.5 us (12%)
  matrix products  13.6 us (9%)
  between operations  13.6 us (9%)
  starting transfers between devices  13.1 us (9%)
  blocking collectives  12.2 us (8%)
    reshape x1, local copies, waits for them, and re-layouts, on_device(): mixing = mixing.reshape(columns * 2 * bins * shots, devices, 2 * bins, held)  20 us
    all_to_all x1, waiting for transfers between devices, on_device(): both = lax.all_to_all(both, ('xline', 'shot'), 0, 0, tiled=True)  19 us
    all_gather x1, waiting for transfers between devices, on_device(): running = lax.all_gather(running, 'xline', axis=0, tiled=True)  15.5 us
    all_to_all x1, blocking collectives, on_device(): running = lax.all_to_all(running, 'shot', 0, 0, tiled=True)  12.2 us
    transpose x1, other arithmetic, on_device(): mixing = jnp.einsum('xqldfsch,fg->dxfslcqgh', mixing, eye).astype(bf16)  9.65 us
    another operation x1, local copies, waits for them, and re-layouts, on_device(): jnp.stack([jnp.stack([real, -imag], 0), jnp.stack([imag, real], 0)], 0)  6.92 us
    dot_general x1, matrix products, on_device(): jnp.einsum('mvph,vphr->mr', mixing, spectra, preferred_element_type=f32)  6.5 us
    all_to_all x1, starting transfers between devices, on_device(): both = lax.all_to_all(both, ('xline', 'shot'), 0, 0, tiled=True)  5.39 us
  transfers between devices with their start and end apart: 4, of which 4 were waited for; matrix products, arithmetic and copies ran while one was open for 4% of the time, Pallas kernels for 0%

profile of v1, /device:TPU:0, one launch (start us, length us, event | category | flops | bytes accessed | tf_op | source)
XLA Modules:
  0.0 149.7 jit_solution(1807389706406463117)
XLA Ops:
  6.5 1.4 broadcast_in_dim.49
  8.0 4.2 %all-to-all-start = ((s32[4,4,16]{2,1,0:T(4,128)}), s32[4,4,16]{2,1,0:T(4,128)S(1)}, u32[]{:S(2)}, u32[]{:S(2)}) async-start(s32[4,4,16]{2,1,0:T(4,128)} %broadcast_in_dim.49), calls=%async_computation | async-start | bytes 16384 | tf_op jit(solution)/shard_map/all_to_all | solution.py:45
  12.5 0.3 fusion.26
  12.8 0.6 select_multiply_fusion
  13.4 2.1 %add_convert_fusion = bf16[64,32,512]{2,1,0:T(8,128)(2,1)} fusion(f32[32,512]{1,0:T(8,128)S(1)} %get-tuple-element.12, f32[64,512]{1,0:T(8,128)S(1)} %get-tuple-element.11, f32[32,512]{1,0:T(8,128)S(1)} %get-tuple-element.10, f32[64,512]{1,0:T(8,128)S(1)} %get-tuple-element.9), kind=kLoop, calls=%fused_computation.3 | loop fusion | flops 4194304 | bytes 2490368 | tf_op jit(solution)/shard_map/convert_element_type | solution.py:31
  15.5 0.5 all-to-all-done
  16.1 0.4 convolution_convert_fusion.2
  16.6 0.7 copy.36
  17.3 3.4 %all-to-all-start.1 = ((bf16[4,64,512]{2,1,0:T(8,128)(2,1)}), bf16[4,64,512]{2,1,0:T(8,128)(2,1)S(1)}, u32[]{:S(2)}, u32[]{:S(2)}) async-start(bf16[4,64,512]{2,1,0:T(8,128)(2,1)} %bitcast.7), calls=%async_computation.1 | async-start | bytes 524288 | tf_op jit(solution)/shard_map/all_to_all | solution.py:54
  20.7 2.8 %convolution_convert_fusion.1 = bf16[512,512]{0,1:T(8,128)(2,1)S(1)} fusion(bf16[512,2048]{1,0:T(8,128)(2,1)S(1)} %bitcast.41, bf16[2048,512]{1,0:T(8,128)(2,1)} %bitcast.42), kind=kOutput, calls=%fused_computation.6 | convolution fusion | flops 1074003968 | bytes 4718592 | tf_op jit(solution)/shard_map/tp,kt->pk/dot_general | solution.py:60
  23.6 3.1 %all-to-all-done.1 = bf16[4,64,512]{2,1,0:T(8,128)(2,1)S(1)} async-done(((bf16[4,64,512]{2,1,0:T(8,128)(2,1)}), bf16[4,64,512]{2,1,0:T(8,128)(2,1)S(1)}, u32[]{:S(2)}, u32[]{:S(2)}) %all-to-all-start.1) | async-done | bytes 262176 | tf_op jit(solution)/shard_map/all_to_all | solution.py:54
  26.7 2.1 %convolution_convert_fusion.3 = bf16[512,64]{0,1:T(8,128)(2,1)S(1)} fusion(bf16[64,2048]{1,0:T(8,128)(2,1)S(1)} %bitcast.47, bf16[2048,512]{1,0:T(8,128)(2,1)} %bitcast.43), kind=kOutput, calls=%fused_computation.10 | convolution fusion | flops 134250496 | bytes 2424832 | tf_op jit(solution)/shard_map/tp,kt->pk/dot_general | solution.py:58
  28.8 1.1 copy.38
  29.9 5.4 %all-to-all-start.2 = ((bf16[32,16,576]{2,1,0:T(8,128)(2,1)}), bf16[32,16,576]{2,1,0:T(8,128)(2,1)S(1)}, u32[]{:S(2)}, u32[]{:S(2)}) async-start(bf16[32,16,576]{2,1,0:T(8,128)(2,1)} %bitcast.9), calls=%async_computation.2 | async-start | bytes 1310720 | tf_op jit(solution)/shard_map/all_to_all | solution.py:66
  35.4 19.0 %all-to-all-done.2 = bf16[32,16,576]{2,1,0:T(8,128)(2,1)S(1)} async-done(((bf16[32,16,576]{2,1,0:T(8,128)(2,1)}), bf16[32,16,576]{2,1,0:T(8,128)(2,1)S(1)}, u32[]{:S(2)}, u32[]{:S(2)}) %all-to-all-start.2) | async-done | bytes 589856 | tf_op jit(solution)/shard_map/all_to_all | solution.py:66
  54.4 0.9 reshape.109
  55.6 0.4 reshape.107
  56.0 1.7 %fusion.31 = (bf16[4,8,1,8,4,8,2]{1,0,6,5,4,3,2:T(4,128)(2,1)}, bf16[1,4,8,8,4,8,2]{2,1,6,5,4,3,0:T(4,128)(2,1)}) fusion(bf16[4,8,2,8,4,8,2]{1,0,6,5,4,3,2:T(4,128)(2,1)S(1)} %reshape.107), kind=kLoop, calls=%fused_computation.54 | loop fusion | bytes 131072 | tf_op jit(solution)/shard_map/slice | solution.py:70
  57.7 2.8 %copy.40 = bf16[4,8,1,8,4,8,2]{5,3,6,4,2,1,0:T(8,128)(2,1)} copy(bf16[4,8,1,8,4,8,2]{1,0,6,5,4,3,2:T(4,128)(2,1)} %get-tuple-element.13) | data formatting | bytes 65536 | tf_op jit(solution)/shard_map/slice | solution.py:70
  60.5 1.8 %copy.41 = bf16[1,4,8,8,4,8,2]{2,1,6,5,4,3,0:T(4,128)(2,1)S(1)} copy(bf16[1,4,8,8,4,8,2]{5,3,6,4,2,1,0:T(8,128)(2,1)} %bitcast.45) | data formatting | bytes 65536 | tf_op jit(solution)/shard_map/squeeze | solution.py:70
  62.3 0.3 neg.21
  62.6 1.4 maximum_bitcast_fusion.1
  64.0 3.1 %maximum_bitcast_fusion = bf16[8,2,2,4,8,4,8,2]{4,3,7,6,5,0,2,1:T(4,128)(2,1)} fusion(bf16[1,2,4,8,8,4,8,2]{3,2,7,6,5,4,1,0:T(4,128)(2,1)S(1)} %get-tuple-element.16, bf16[1,2,4,8,8,4,8,2]{3,2,7,6,5,4,1,0:T(4,128)(2,1)S(1)} %get-tuple-element.15), kind=kLoop, calls=%fused_computation.4 | loop fusion | flops 65536 | bytes 262144 | tf_op jit(solution)/shard_map/stack | solution.py:71
  67.1 6.9 %copy.43 = bf16[8,2,2,4,8,4,8,2]{6,3,2,7,5,0,1,4:T(4,128)(2,1)} copy(bf16[8,2,2,4,8,4,8,2]{4,3,7,6,5,0,2,1:T(4,128)(2,1)} %maximum_bitcast_fusion) | data formatting | bytes 262144 | tf_op jit(solution)/shard_map/stack | solution.py:71
  74.0 9.6 %multiply_bitcast_fusion = bf16[8,2,8,4,4,8,2,8,2]{5,4,7,6,8,3,2,1,0:T(4,128)(2,1)} fusion(bf16[8,2,2,4,8,4,8,2]{6,3,2,7,5,0,1,4:T(4,128)(2,1)} %copy.43, bf16[8,8]{1,0:T(8,128)(2,1)S(1)} %fusion.28), kind=kLoop, calls=%fused_computation | loop fusion | flops 524288 | bytes 1179776 | tf_op jit(solution)/shard_map/xqldfsch,fg->dxfslcqgh/transpose | solution.py:75
  83.7 20.0 %reshape.108 = bf16[512,32,16,2]{1,2,3,0:T(8,128)(2,1)} reshape(bf16[8,2,8,4,4,8,2,8,2]{5,4,7,6,8,3,2,1,0:T(4,128)(2,1)} %multiply_bitcast_fusion) | data formatting | bytes 2097152 | tf_op jit(solution)/shard_map/reshape | solution.py:76
  103.7 6.5 %fusion.5 = bf16[512,256]{1,0:T(8,128)(2,1)S(1)} fusion(bf16[512,32,16,2]{1,2,3,0:T(8,128)(2,1)} %reshape.108, bf16[32,16,2,256]{3,2,1,0:T(2,128)(2,1)S(1)} %copy-done.3), kind=kOutput, calls=%fused_computation.8 | convolution fusion | flops 268566528 | bytes 1835008 | tf_op jit(solution)/shard_map/mvph,vphr->mr/dot_general | solution.py:77
  110.2 12.2 %all_to_all.20 = bf16[8,64,256]{2,1,0:T(8,128)(2,1)} all-to-all(bf16[8,64,256]{2,1,0:T(8,128)(2,1)S(1)} %bitcast.49), channel_id=1, replica_groups=mesh['shot'=8,'xline'=4] {'shot'}, dimensions={0} | all-to-all | bytes 524288 | tf_op jit(solution)/shard_map/all_to_all | solution.py:81
  122.4 15.5 %all-gather.2.cloned.1.call-done = bf16[32,64,256]{2,1,0:T(8,128)(2,1)} async-done(((bf16[8,64,256]{2,1,0:T(8,128)(2,1)}), bf16[32,64,256]{2,1,0:T(8,128)(2,1)}) %all-gather.2.cloned.1.call-update) | async-done | bytes 1048592 | tf_op jit(solution)/shard_map/all_gather | solution.py:82
  137.9 1.3 reshape.111
  139.3 1.8 %convolution_convert_fusion = bf16[512,4,256]{2,0,1:T(8,128)(2,1)S(1)} fusion(bf16[512,4,256]{2,1,0:T(4,128)(2,1)S(1)} %reshape.111, bf16[2048,512]{1,0:T(8,128)(2,1)} %bitcast.44, s32[]{:T(128)S(6)} %select_n.31), kind=kOutput, calls=%fused_computation.5 | convolution fusion | flops 538443776 | bytes 2621444 | tf_op jit(solution)/shard_map/tp,psr->tsr/dot_general | solution.py:86
  141.0 1.8 %copy.47 = bf16[512,4,256]{2,1,0:T(4,128)(2,1)} copy(bf16[512,4,256]{2,0,1:T(8,128)(2,1)S(1)} %convolution_convert_fusion) | data formatting | bytes 2097152 | tf_op jit(solution)/shard_map/convert_element_type | solution.py:87
  (24 shorter events, 0.7 us)
Async XLA Ops:
  6.5 14.2 %copy-start = (bf16[1,2,256,2048]{3,2,1,0:T(8,128)(2,1)S(1)}, bf16[1,2,256,2048]{3,2,1,0:T(8,128)(2,1)}, u32[]{:S(2)}) copy-start(bf16[1,2,256,2048]{3,2,1,0:T(8,128)(2,1)} %param.3) | copy-start | bytes 6291460
  6.5 9.6 %copy-start.2 = (bf16[512,4,256]{2,1,0:T(4,128)(2,1)S(1)}, bf16[512,4,256]{2,1,0:T(4,128)(2,1)}, u32[]{:S(2)}) copy-start(bf16[512,4,256]{2,1,0:T(4,128)(2,1)} %param.4) | copy-start | bytes 3145732
  8.0 8.1 %all-to-all-start = ((s32[4,4,16]{2,1,0:T(4,128)}), s32[4,4,16]{2,1,0:T(4,128)S(1)}, u32[]{:S(2)}, u32[]{:S(2)}) async-start(s32[4,4,16]{2,1,0:T(4,128)} %broadcast_in_dim.49), calls=%async_computation | async-start | bytes 16384 | tf_op jit(solution)/shard_map/all_to_all | solution.py:45
  17.3 9.4 %all-to-all-start.1 = ((bf16[4,64,512]{2,1,0:T(8,128)(2,1)}), bf16[4,64,512]{2,1,0:T(8,128)(2,1)S(1)}, u32[]{:S(2)}, u32[]{:S(2)}) async-start(bf16[4,64,512]{2,1,0:T(8,128)(2,1)} %bitcast.7), calls=%async_computation.1 | async-start | bytes 524288 | tf_op jit(solution)/shard_map/all_to_all | solution.py:54
  29.9 24.4 %all-to-all-start.2 = ((bf16[32,16,576]{2,1,0:T(8,128)(2,1)}), bf16[32,16,576]{2,1,0:T(8,128)(2,1)S(1)}, u32[]{:S(2)}, u32[]{:S(2)}) async-start(bf16[32,16,576]{2,1,0:T(8,128)(2,1)} %bitcast.9), calls=%async_computation.2 | async-start | bytes 1310720 | tf_op jit(solution)/shard_map/all_to_all | solution.py:66
  35.3 102.6 %all-gather.2.cloned.1.call-start = ((), (), s32[]{:S(2)}) async-start(), calls=%async_computation.4 | async-start | bytes 1310720 | tf_op jit(solution)/shard_map/all_gather | solution.py:82
  57.7 4.9 %copy-start.1 = (bf16[1,4,8,8,4,8,2]{2,1,6,5,4,3,0:T(4,128)(2,1)S(1)}, bf16[1,4,8,8,4,8,2]{2,1,6,5,4,3,0:T(4,128)(2,1)}, u32[]{:S(2)}) copy-start(bf16[1,4,8,8,4,8,2]{2,1,6,5,4,3,0:T(4,128)(2,1)} %get-tuple-element.14) | copy-start | bytes 98308
  83.7 20.0 %copy-start.3 = (bf16[32,16,2,256]{3,2,1,0:T(2,128)(2,1)S(1)}, bf16[32,16,2,256]{3,2,1,0:T(2,128)(2,1)}, u32[]{:S(2)}) copy-start(bf16[32,16,2,256]{3,2,1,0:T(2,128)(2,1)} %reshape.109) | copy-start | bytes 1572868
Sparse Core Ops, SparseCore 0:
  122.5 15.3 all-gather.1

commit v2 on v1

--- a/solution.py
+++ b/solution.py
@@ -1,8 +1,11 @@
+import functools
 import math
 
 import jax
 import jax.numpy as jnp
 from jax import lax
+from jax.experimental import pallas as pl
+from jax.experimental.pallas import tpu as pltpu
 from jax.sharding import PartitionSpec as P
 
 NT = 2048
@@ -29,6 +32,51 @@
     first, second, cos_lo, sin_lo = lax.optimization_barrier((first, second, cos_lo, sin_lo))
     table = first[:, None] * cos_lo[None] + second[:, None] * sin_lo[None]
     return table.reshape(NT, 2 * NF).astype(jnp.bfloat16)
+
+
+def mix_kernel(lines, columns, held, bins, shots, spectra_ref, picked_ref, out_ref):
+    gathers = columns * held
+    receivers = out_ref.shape[1]
+    rows = columns * bins
+    depth = columns * 2 * bins
+    taken = 2 * shots * gathers
+    wide = held * depth
+
+    k = lax.broadcasted_iota(jnp.int32, (taken, wide), 0)
+    j = lax.broadcasted_iota(jnp.int32, (taken, wide), 1)
+    k_imag, k_shot, k_gather = k // (shots * gathers), k // gathers % shots, k % gathers
+    j_held, j_column, j_imag = j // depth, j % depth // (2 * bins), j // bins % 2
+    same = k_gather == j_column * held + j_held
+    crossed = k_imag != j_imag
+    expand = []
+    for shot in range(shots):
+        for part in range(2):
+            hit = same & (k_shot == shot) & (crossed if part else ~crossed)
+            value = jnp.where(hit, 1.0, 0.0)
+            if part == 0:
+                value = jnp.where(j_imag == 1, -value, value)
+            expand.append(value.astype(jnp.bfloat16))
+    bin_of_row = lax.broadcasted_iota(jnp.int32, (rows, wide), 0) % bins
+    bin_of_column = lax.broadcasted_iota(jnp.int32, (rows, wide), 1) % bins
+    same_bin = bin_of_row == bin_of_column
+
+    total = jnp.zeros(out_ref.shape, jnp.float32)
+    for line in range(lines):
+        block = picked_ref[line * rows : (line + 1) * rows, :]
+        mixing = [
+            jnp.where(
+                same_bin, jnp.dot(block, matrix, preferred_element_type=jnp.float32), 0.0
+            ).astype(jnp.bfloat16)
+            for matrix in expand
+        ]
+        held_rows = slice(line * depth, (line + 1) * depth)
+        spectra = jnp.concatenate(
+            [spectra_ref[held_rows, h * receivers : (h + 1) * receivers] for h in range(held)], axis=0
+        )
+        total += jnp.dot(
+            jnp.concatenate(mixing, axis=0), spectra, preferred_element_type=jnp.float32
+        )
+    out_ref[...] = total.astype(out_ref.dtype)
 
 
 def on_device(records, targets, aperture):
@@ -61,26 +109,23 @@
         "tp,kt->pk", table, records.reshape(held * receivers, NT), preferred_element_type=f32
     ).astype(bf16)
 
-    width = held * receivers
-    both = jnp.concatenate([spectra, picked], axis=1).reshape(devices, 2 * bins, -1)
-    both = lax.all_to_all(both, ("xline", "shot"), 0, 0, tiled=True)
-    spectra = both[:, :, :width].reshape(devices, 2 * bins, held, receivers)
-    picked = both[:, :, width:].reshape(lines, columns, 2, bins, shots, columns, held)
+    spectra = spectra.reshape(devices, 2 * bins, held * receivers)
+    spectra = lax.all_to_all(spectra, ("xline", "shot"), 0, 0, tiled=True)
+    picked = picked.reshape(devices, 2, bins, shots * gathers)
+    picked = jnp.concatenate([picked[:, 0], picked[:, 1]], axis=-1)
+    picked = lax.all_to_all(picked, ("xline", "shot"), 0, 0, tiled=True)
 
-    real, imag = picked[:, :, 0], picked[:, :, 1]
-    mixing = jnp.stack(
-        [jnp.stack([real, -imag], 0), jnp.stack([imag, real], 0)], 0
-    )
-    eye = jnp.eye(bins, dtype=bf16)
-    mixing = jnp.einsum("xqldfsch,fg->dxfslcqgh", mixing, eye).astype(bf16)
-    mixing = mixing.reshape(columns * 2 * bins * shots, devices, 2 * bins, held)
-    running = jnp.einsum(
-        "mvph,vphr->mr", mixing, spectra, preferred_element_type=f32
-    ).astype(bf16)
-    running = running.reshape(columns, 2 * bins * shots, receivers)
+    running = pl.pallas_call(
+        functools.partial(mix_kernel, lines, columns, held, bins, shots),
+        out_shape=jax.ShapeDtypeStruct((shots * 2 * columns * bins, receivers), bf16),
+        in_specs=[pl.BlockSpec(memory_space=pltpu.VMEM)] * 2,
+        out_specs=pl.BlockSpec(memory_space=pltpu.VMEM),
+    )(spectra.reshape(2 * NF, held * receivers), picked.reshape(NF, -1))
+    running = running.reshape(shots, 2, columns, bins, receivers).transpose(2, 0, 1, 3, 4)
+    running = running.reshape(columns, shots, 2 * bins, receivers)
     running = lax.all_to_all(running, "shot", 0, 0, tiled=True)
     running = lax.all_gather(running, "xline", axis=0, tiled=True)
-    running = running.reshape(2 * NF, shots, receivers)
+    running = running.transpose(0, 2, 1, 3).reshape(2 * NF, shots, receivers)
 
     rows = lax.dynamic_slice_in_dim(table, lax.axis_index("xline") * time_rows, time_rows, 0)
     out = jnp.einsum("tp,psr->tsr", rows * 2, running, preferred_element_type=f32)

time: 151 us -> 106 us (0.70)
  local copies, waits for them, and re-layouts: 41.5 us -> 6.68 us
  blocking collectives: 12.2 us -> 30.8 us
  other arithmetic: 17.5 us -> 3.7 us
  waiting for transfers between devices: 38.2 us -> 26.4 us
  matrix products: 13.6 us -> 8.37 us
  Pallas kernels: 0 us -> 2.65 us
    reshape x4 -> x1, local copies, waits for them, and re-layouts: 22.7 us -> 0.97 us  [on_device(): running.reshape(shots, 2, columns, bins, receivers).transpose(2, 0, 1, 3, 4)]
    all_to_all x0 -> x1, blocking collectives: none -> 18.6 us  [on_device(): spectra = lax.all_to_all(spectra, ('xline', 'shot'), 0, 0, tiled=True)]
    all_to_all x1, waiting for transfers between devices: 19 us -> 4.32 us  [on_device(): picked = lax.all_to_all(picked, ('xline', 'shot'), 0, 0, tiled=True)]
    transpose x1 -> x0, other arithmetic: 9.65 us -> none  [on_device(): mixing = jnp.einsum('xqldfsch,fg->dxfslcqgh', mixing, eye).astype(bf16)]
    another operation x1 -> x0, local copies, waits for them, and re-layouts: 6.92 us -> none  [on_device(): jnp.stack([jnp.stack([real, -imag], 0), jnp.stack([imag, real], 0)], 0)]
    dot_general x1 -> x0, matrix products: 6.5 us -> none  [on_device(): jnp.einsum('mvph,vphr->mr', mixing, spectra, preferred_element_type=f32)]
    slice x5 -> x0, local copies, waits for them, and re-layouts: 4.78 us -> none  [the longest x2 4.49 us: on_device(): real, imag = (picked[:, :, 0], picked[:, :, 1])]
    another operation x3 -> x0, other arithmetic: 4.51 us -> none  [the longest x2 4.5 us: on_device(): jnp.stack([jnp.stack([real, -imag], 0), jnp.stack([imag, real], 0)], 0)]
  transfers between devices with their start and end apart: 4 -> 4, of which waited for: 4 -> 4; matrix products, arithmetic and copies ran while one was open for 4% -> 6% of each run, Pallas kernels for 0% -> 0%
where the time goes in v2:
time: 106 us; the launch traced here: 105 us
  blocking collectives  30.8 us (29%)
  waiting for transfers between devices  26.4 us (25%)
  between operations  13.5 us (13%)
  starting transfers between devices  13.1 us (12%)
  matrix products  8.37 us (8%)
  local copies, waits for them, and re-layouts  6.68 us (6%)
  other arithmetic  3.7 us (3%)
  Pallas kernels  2.65 us (2%)
    all_to_all x1, blocking collectives, on_device(): spectra = lax.all_to_all(spectra, ('xline', 'shot'), 0, 0, tiled=True)  18.6 us
    all_gather x1, waiting for transfers between devices, on_device(): running = lax.all_gather(running, 'xline', axis=0, tiled=True)  15.5 us
    all_to_all x1, blocking collectives, on_device(): running = lax.all_to_all(running, 'shot', 0, 0, tiled=True)  12.2 us
    all_to_all x1, starting transfers between devices, on_device(): picked = lax.all_to_all(picked, ('xline', 'shot'), 0, 0, tiled=True)  5.38 us
    all_to_all x1, waiting for transfers between devices, on_device(): picked = lax.all_to_all(picked, ('xline', 'shot'), 0, 0, tiled=True)  4.32 us
    all_to_all x1, starting transfers between devices, on_device(): lax.all_to_all(jnp.broadcast_to(aperture.reshape(1, shots, gathers), (lin...  4.24 us
    all_to_all x1, waiting for transfers between devices, on_device(): lax.all_to_all(traces.reshape(lines, shots * gathers, time_rows), 'xline'...  3.92 us
    all_to_all x1, starting transfers between devices, on_device(): lax.all_to_all(traces.reshape(lines, shots * gathers, time_rows), 'xline'...  3.41 us
  transfers between devices with their start and end apart: 4, of which 4 were waited for; matrix products, arithmetic and copies ran while one was open for 6% of the time, Pallas kernels for 0%

profile of v2, /device:TPU:0, one launch (start us, length us, event | category | flops | bytes accessed | tf_op | source)
XLA Modules:
  0.0 105.2 jit_solution(1596108714604334187)
XLA Ops:
  6.5 0.0 copy-start
  6.5 1.4 %broadcast_in_dim.49 = s32[4,4,16]{2,1,0:T(4,128)} broadcast(s32[4,16]{1,0:T(4,128)} %bitcast.53), dimensions={1,2} | broadcast | bytes 1280 | tf_op jit(solution)/shard_map/broadcast_in_dim | solution.py:94
  8.0 4.2 %all-to-all-start.1 = ((s32[4,4,16]{2,1,0:T(4,128)}), s32[4,4,16]{2,1,0:T(4,128)S(1)}, u32[]{:S(2)}, u32[]{:S(2)}) async-start(s32[4,4,16]{2,1,0:T(4,128)} %broadcast_in_dim.49), calls=%async_computation.1 | async-start | bytes 16384 | tf_op jit(solution)/shard_map/all_to_all | solution.py:93
  12.3 0.1 mul.144
  12.4 0.1 eq.39
  12.5 0.6 select_multiply_fusion
  13.1 0.3 fusion.16
  13.4 2.7 %all-to-all-done.1 = s32[4,4,16]{2,1,0:T(4,128)S(1)} async-done(((s32[4,4,16]{2,1,0:T(4,128)}), s32[4,4,16]{2,1,0:T(4,128)S(1)}, u32[]{:S(2)}, u32[]{:S(2)}) %all-to-all-start.1) | async-done | bytes 1056 | tf_op jit(solution)/shard_map/all_to_all | solution.py:93
  16.0 0.1 eq.40
  16.1 1.7 %convolution_convert_fusion.2 = bf16[4,64,512]{2,1,0:T(8,128)(2,1)S(1)} fusion(bf16[512,4,256]{2,1,0:T(4,128)(2,1)} %param.4, s32[4,64]{1,0:T(4,128)S(1)} %eq.40), kind=kOutput, calls=%fused_computation.3 | convolution fusion | flops 67305472 | bytes 1311744 | tf_op jit(solution)/shard_map/skr,tsr->skt/dot_general | solution.py:100
  17.8 0.7 copy.26
  18.5 3.4 %all-to-all-start.2 = ((bf16[4,64,512]{2,1,0:T(8,128)(2,1)}), bf16[4,64,512]{2,1,0:T(8,128)(2,1)S(1)}, u32[]{:S(2)}, u32[]{:S(2)}) async-start(bf16[4,64,512]{2,1,0:T(8,128)(2,1)} %bitcast.9), calls=%async_computation.2 | async-start | bytes 524288 | tf_op jit(solution)/shard_map/all_to_all | solution.py:102
  21.9 2.1 %add_convert_fusion = bf16[64,32,512]{2,1,0:T(8,128)(2,1)} fusion(f32[32,512]{1,0:T(8,128)S(1)} %get-tuple-element.12, f32[64,512]{1,0:T(8,128)S(1)} %get-tuple-element.11, f32[32,512]{1,0:T(8,128)S(1)} %get-tuple-element.10, f32[64,512]{1,0:T(8,128)S(1)} %get-tuple-element.9), kind=kLoop, calls=%fused_computation | loop fusion | flops 4194304 | bytes 2490368 | tf_op jit(solution)/shard_map/convert_element_type | solution.py:34
  24.0 3.9 %all-to-all-done.2 = bf16[4,64,512]{2,1,0:T(8,128)(2,1)S(1)} async-done(((bf16[4,64,512]{2,1,0:T(8,128)(2,1)}), bf16[4,64,512]{2,1,0:T(8,128)(2,1)S(1)}, u32[]{:S(2)}, u32[]{:S(2)}) %all-to-all-start.2) | async-done | bytes 262176 | tf_op jit(solution)/shard_map/all_to_all | solution.py:102
  27.9 2.1 %convolution_convert_fusion.3 = bf16[512,64]{0,1:T(8,128)(2,1)S(1)} fusion(bf16[64,2048]{1,0:T(8,128)(2,1)S(1)} %bitcast.43, bf16[2048,512]{1,0:T(8,128)(2,1)} %bitcast.38), kind=kOutput, calls=%fused_computation.4 | convolution fusion | flops 134250496 | bytes 2424832 | tf_op jit(solution)/shard_map/tp,kt->pk/dot_general | solution.py:106
  30.0 0.1 copy.28
  30.1 0.7 pad_maximum_fusion
  30.9 5.4 %all-to-all-start.3 = ((bf16[32,8,128]{2,1,0:T(8,128)(2,1)}), bf16[32,8,128]{2,1,0:T(8,128)(2,1)S(1)}, u32[]{:S(2)}, u32[]{:S(2)}) async-start(bf16[32,8,128]{2,1,0:T(8,128)(2,1)} %pad_maximum_fusion), calls=%async_computation.3 | async-start | bytes 131072 | tf_op jit(solution)/shard_map/all_to_all | solution.py:116
  36.2 0.0 all-gather.2.cloned.1.call-start
  36.3 0.0 copy-done
  36.3 2.9 %convolution_convert_fusion.1 = bf16[512,512]{1,0:T(8,128)(2,1)S(1)} fusion(bf16[2048,512]{1,0:T(8,128)(2,1)} %bitcast.39, bf16[512,2048]{1,0:T(8,128)(2,1)S(1)} %bitcast.37), kind=kOutput, calls=%fused_computation.2 | convolution fusion | flops 1074003968 | bytes 4718592 | tf_op jit(solution)/shard_map/tp,kt->pk/dot_general | solution.py:108
  39.2 4.3 %all-to-all-done.3 = bf16[32,8,128]{2,1,0:T(8,128)(2,1)S(1)} async-done(((bf16[32,8,128]{2,1,0:T(8,128)(2,1)}), bf16[32,8,128]{2,1,0:T(8,128)(2,1)S(1)}, u32[]{:S(2)}, u32[]{:S(2)}) %all-to-all-start.3) | async-done | bytes 65568 | tf_op jit(solution)/shard_map/all_to_all | solution.py:116
  43.5 18.6 %all_to_all.25 = bf16[32,16,512]{2,1,0:T(8,128)(2,1)} all-to-all(bf16[32,16,512]{2,1,0:T(8,128)(2,1)S(1)} %bitcast.49), channel_id=1, replica_groups=mesh['shot'=8,'xline'=4] {'xline','shot'}, dimensions={0} | all-to-all | bytes 1048576 | tf_op jit(solution)/shard_map/all_to_all | solution.py:113
  62.1 0.0 copy-done.1
  62.1 2.6 %shard_map.37 = bf16[512,256]{1,0:T(8,128)(2,1)} custom-call(bf16[512,512]{1,0:T(8,128)(2,1)} %bitcast.41, bf16[256,128]{1,0:T(8,128)(2,1)} %bitcast.51), custom_call_target="tpu_custom_call" | custom-call | tf_op jit(solution)/shard_map/pallas_call | solution.py:118
  64.8 1.0 copy.38
  65.8 12.2 %all_to_all.26 = bf16[8,4,16,256]{3,2,1,0:T(8,128)(2,1)} all-to-all(bf16[8,4,16,256]{3,2,1,0:T(8,128)(2,1)S(1)} %bitcast.48), channel_id=1, replica_groups=mesh['shot'=8,'xline'=4] {'shot'}, dimensions={0} | all-to-all | bytes 524288 | tf_op jit(solution)/shard_map/all_to_all | solution.py:126
  78.0 0.0 all-gather.2.cloned.1.call-update
  78.0 15.5 %all-gather.2.cloned.1.call-done = bf16[32,4,16,256]{3,2,1,0:T(8,128)(2,1)} async-done(((bf16[8,4,16,256]{3,2,1,0:T(8,128)(2,1)}), bf16[32,4,16,256]{3,2,1,0:T(8,128)(2,1)}) %all-gather.2.cloned.1.call-update) | async-done | bytes 1048592 | tf_op jit(solution)/shard_map/all_gather | solution.py:127
  93.5 1.3 %copy.31 = bf16[32,16,4,256]{3,1,0,2:T(8,128)(2,1)S(1)} copy(bf16[32,16,4,256]{3,1,2,0:T(8,128)(2,1)} %bitcast.44) | data formatting | bytes 2097152 | tf_op jit(solution)/shard_map/transpose | solution.py:128
  94.8 1.8 %convolution_convert_fusion = bf16[512,4,256]{2,0,1:T(8,128)(2,1)S(1)} fusion(bf16[512,4,256]{2,0,1:T(8,128)(2,1)S(1)} %bitcast.45, bf16[2048,512]{1,0:T(8,128)(2,1)} %bitcast.40, s32[]{:T(128)S(6)} %select_n.31), kind=kOutput, calls=%fused_computation.1 | convolution fusion | flops 538443776 | bytes 2621444 | tf_op jit(solution)/shard_map/tp,psr->tsr/dot_general | solution.py:131
  96.6 1.8 %copy.32 = bf16[512,4,256]{2,1,0:T(4,128)(2,1)} copy(bf16[512,4,256]{2,0,1:T(8,128)(2,1)S(1)} %convolution_convert_fusion) | data formatting | bytes 2097152 | tf_op jit(solution)/shard_map/convert_element_type | solution.py:132
  (8 shorter events, 0.1 us)
Async XLA Ops:
  6.5 29.8 %copy-start = (bf16[1,2,256,2048]{3,2,1,0:T(8,128)(2,1)S(1)}, bf16[1,2,256,2048]{3,2,1,0:T(8,128)(2,1)}, u32[]{:S(2)}) copy-start(bf16[1,2,256,2048]{3,2,1,0:T(8,128)(2,1)} %param.3) | copy-start | bytes 6291460
  8.0 8.1 %all-to-all-start.1 = ((s32[4,4,16]{2,1,0:T(4,128)}), s32[4,4,16]{2,1,0:T(4,128)S(1)}, u32[]{:S(2)}, u32[]{:S(2)}) async-start(s32[4,4,16]{2,1,0:T(4,128)} %broadcast_in_dim.49), calls=%async_computation.1 | async-start | bytes 16384 | tf_op jit(solution)/shard_map/all_to_all | solution.py:93
  18.5 9.4 %all-to-all-start.2 = ((bf16[4,64,512]{2,1,0:T(8,128)(2,1)}), bf16[4,64,512]{2,1,0:T(8,128)(2,1)S(1)}, u32[]{:S(2)}, u32[]{:S(2)}) async-start(bf16[4,64,512]{2,1,0:T(8,128)(2,1)} %bitcast.9), calls=%async_computation.2 | async-start | bytes 524288 | tf_op jit(solution)/shard_map/all_to_all | solution.py:102
  30.9 12.7 %all-to-all-start.3 = ((bf16[32,8,128]{2,1,0:T(8,128)(2,1)}), bf16[32,8,128]{2,1,0:T(8,128)(2,1)S(1)}, u32[]{:S(2)}, u32[]{:S(2)}) async-start(bf16[32,8,128]{2,1,0:T(8,128)(2,1)} %pad_maximum_fusion), calls=%async_computation.3 | async-start | bytes 131072 | tf_op jit(solution)/shard_map/all_to_all | solution.py:116
  36.2 57.3 %all-gather.2.cloned.1.call-start = ((), (), s32[]{:S(2)}) async-start(), calls=%async_computation.5 | async-start | bytes 1310720 | tf_op jit(solution)/shard_map/all_gather | solution.py:127
  43.5 18.6 %copy-start.1 = (bf16[32,8,128]{2,1,0:T(8,128)(2,1)}, bf16[32,8,128]{2,1,0:T(8,128)(2,1)S(1)}, u32[]{:S(2)}) copy-start(bf16[32,8,128]{2,1,0:T(8,128)(2,1)S(1)} %all-to-all-done.3) | copy-start | bytes 196612
Sparse Core Ops, SparseCore 0:
  78.1 15.3 all-gather.1

commit v3 on v2

--- a/solution.py
+++ b/solution.py
@@ -79,6 +79,165 @@
     out_ref[...] = total.astype(out_ref.dtype)
 
 
+def spread_kernel(lines, columns, spectra_ref, picked_ref, spectra_out, picked_out, send, recv, own):
+    devices = lines * columns
+    me = lax.axis_index("xline") * columns + lax.axis_index("shot")
+    mesh_id = pl.DeviceIdType.MESH
+    barrier = pltpu.get_barrier_semaphore()
+
+    def greet(step, _):
+        peer = lax.rem(me + step, devices)
+        pl.semaphore_signal(
+            barrier, inc=1,
+            device_id={"xline": peer // columns, "shot": lax.rem(peer, columns)},
+            device_id_type=mesh_id,
+        )
+        return 0
+
+    lax.fori_loop(1, devices, greet, 0)
+    pl.semaphore_wait(barrier, devices - 1)
+
+    def copies(step):
+        peer = lax.rem(me + step, devices)
+        return [
+            pltpu.make_async_remote_copy(
+                src_ref=source.at[peer],
+                dst_ref=target.at[me],
+                send_sem=send.at[which, step],
+                recv_sem=recv.at[which, step],
+                device_id={"xline": peer // columns, "shot": lax.rem(peer, columns)},
+                device_id_type=mesh_id,
+            )
+            for which, (source, target) in enumerate(
+                ((spectra_ref, spectra_out), (picked_ref, picked_out))
+            )
+        ]
+
+    def begin(step, _):
+        for copy in copies(step):
+            copy.start()
+        return 0
+
+    def finish(step, _):
+        for copy in copies(step):
+            copy.wait_send()
+        origin = lax.rem(me + devices - step, devices)
+        for which, target in enumerate((spectra_out, picked_out)):
+            pltpu.make_async_remote_copy(
+                src_ref=target.at[origin],
+                dst_ref=target.at[origin],
+                send_sem=send.at[which, step],
+                recv_sem=recv.at[which, step],
+                device_id={"xline": origin // columns, "shot": lax.rem(origin, columns)},
+                device_id_type=mesh_id,
+            ).wait_recv()
+        return 0
+
+    lax.fori_loop(1, devices, begin, 0)
+    mine = [
+        pltpu.make_async_copy(spectra_ref.at[me], spectra_out.at[me], own.at[0]),
+        pltpu.make_async_copy(picked_ref.at[me], picked_out.at[me], own.at[1]),
+    ]
+    for copy in mine:
+        copy.start()
+    for copy in mine:
+        copy.wait()
+    lax.fori_loop(1, devices, finish, 0)
+
+
+def collect_kernel(lines, columns, running_ref, out_ref, send, recv, own):
+    line = lax.axis_index("xline")
+    me = lax.axis_index("shot")
+    core_line = line + 1 - 2 * lax.rem(line, 2)
+    far_line = lax.rem(line + lines // 2, lines)
+    diagonal_line = lax.rem(core_line + lines // 2, lines)
+    mesh_id = pl.DeviceIdType.MESH
+    barrier = pltpu.get_barrier_semaphore()
+
+    def greet(step, _):
+        pl.semaphore_signal(
+            barrier, inc=1, device_id={"shot": lax.rem(me + step, columns)}, device_id_type=mesh_id
+        )
+        return 0
+
+    lax.fori_loop(1, columns, greet, 0)
+    for peer in (core_line, far_line):
+        pl.semaphore_signal(barrier, inc=1, device_id={"xline": peer}, device_id_type=mesh_id)
+    pl.semaphore_wait(barrier, columns + 1)
+
+    def across(step):
+        peer = lax.rem(me + step, columns)
+        return pltpu.make_async_remote_copy(
+            src_ref=running_ref.at[peer],
+            dst_ref=out_ref.at[line * columns + me],
+            send_sem=send.at[0, step],
+            recv_sem=recv.at[0, step],
+            device_id={"shot": peer},
+            device_id_type=mesh_id,
+        )
+
+    def onward(stage, source_line, peer_line, step):
+        slot = source_line * columns + lax.rem(me + columns - step, columns)
+        return pltpu.make_async_remote_copy(
+            src_ref=out_ref.at[slot],
+            dst_ref=out_ref.at[slot],
+            send_sem=send.at[stage, step],
+            recv_sem=recv.at[stage, step],
+            device_id={"xline": peer_line},
+            device_id_type=mesh_id,
+        )
+
+    def begin(step, _):
+        across(step).start()
+        return 0
+
+    lax.fori_loop(1, columns, begin, 0)
+    mine = pltpu.make_async_copy(running_ref.at[me], out_ref.at[line * columns + me], own.at[0])
+    mine.start()
+    mine.wait()
+    onward(2, line, far_line, 0).start()
+    onward(1, line, core_line, 0).start()
+
+    def relay(step, _):
+        slot = line * columns + lax.rem(me + columns - step, columns)
+        pltpu.make_async_remote_copy(
+            src_ref=out_ref.at[slot],
+            dst_ref=out_ref.at[slot],
+            send_sem=send.at[0, step],
+            recv_sem=recv.at[0, step],
+            device_id={"shot": lax.rem(me + columns - step, columns)},
+            device_id_type=mesh_id,
+        ).wait_recv()
+        onward(2, line, far_line, step).start()
+        onward(1, line, core_line, step).start()
+        return 0
+
+    lax.fori_loop(1, columns, relay, 0)
+
+    def turn(step, _):
+        onward(2, far_line, far_line, step).wait_recv()
+        onward(3, far_line, core_line, step).start()
+        return 0
+
+    lax.fori_loop(0, columns, turn, 0)
+
+    def finish(step, _):
+        onward(1, core_line, core_line, step).wait_recv()
+        onward(3, diagonal_line, core_line, step).wait_recv()
+        onward(1, line, core_line, step).wait_send()
+        onward(2, line, far_line, step).wait_send()
+        onward(3, far_line, core_line, step).wait_send()
+        return 0
+
+    lax.fori_loop(0, columns, finish, 0)
+
+    def sent(step, _):
+        across(step).wait_send()
+        return 0
+
+    lax.fori_loop(1, columns, sent, 0)
+
+
 def on_device(records, targets, aperture):
     f32, bf16 = jnp.float32, jnp.bfloat16
     lines = lax.axis_size("xline")
@@ -110,10 +269,21 @@
     ).astype(bf16)
 
     spectra = spectra.reshape(devices, 2 * bins, held * receivers)
-    spectra = lax.all_to_all(spectra, ("xline", "shot"), 0, 0, tiled=True)
     picked = picked.reshape(devices, 2, bins, shots * gathers)
     picked = jnp.concatenate([picked[:, 0], picked[:, 1]], axis=-1)
-    picked = lax.all_to_all(picked, ("xline", "shot"), 0, 0, tiled=True)
+    in_vmem = pl.BlockSpec(memory_space=pltpu.VMEM)
+    dma = pltpu.SemaphoreType.DMA
+    spectra, picked = pl.pallas_call(
+        functools.partial(spread_kernel, lines, columns),
+        out_shape=[
+            jax.ShapeDtypeStruct(spectra.shape, bf16),
+            jax.ShapeDtypeStruct(picked.shape, bf16),
+        ],
+        in_specs=[in_vmem] * 2,
+        out_specs=[in_vmem] * 2,
+        scratch_shapes=[dma((2, devices)), dma((2, devices)), dma((2,))],
+        compiler_params=pltpu.CompilerParams(collective_id=0, has_side_effects=True),
+    )(spectra, picked)
 
     running = pl.pallas_call(
         functools.partial(mix_kernel, lines, columns, held, bins, shots),
@@ -123,8 +293,14 @@
     )(spectra.reshape(2 * NF, held * receivers), picked.reshape(NF, -1))
     running = running.reshape(shots, 2, columns, bins, receivers).transpose(2, 0, 1, 3, 4)
     running = running.reshape(columns, shots, 2 * bins, receivers)
-    running = lax.all_to_all(running, "shot", 0, 0, tiled=True)
-    running = lax.all_gather(running, "xline", axis=0, tiled=True)
+    running = pl.pallas_call(
+        functools.partial(collect_kernel, lines, columns),
+        out_shape=jax.ShapeDtypeStruct((devices, *running.shape[1:]), bf16),
+        in_specs=[in_vmem],
+        out_specs=in_vmem,
+        scratch_shapes=[dma((4, columns)), dma((4, columns)), dma((1,))],
+        compiler_params=pltpu.CompilerParams(collective_id=1, has_side_effects=True),
+    )(running)
     running = running.transpose(0, 2, 1, 3).reshape(2 * NF, shots, receivers)
 
     rows = lax.dynamic_slice_in_dim(table, lax.axis_index("xline") * time_rows, time_rows, 0)

time: 106 us -> 71.4 us (0.67)
  Pallas kernels: 2.65 us -> 41.3 us
  blocking collectives: 30.8 us -> 0 us
  waiting for transfers between devices: 26.4 us -> 2.83 us
  between operations: 13.5 us -> 0.11 us
  starting transfers between devices: 13.1 us -> 7.64 us
    pallas_call x0 -> x2, Pallas kernels: none -> 38.6 us  [the longest x1 21.1 us: on_device(): pl.pallas_call(functools.partial(spread_kernel, lines, columns), out_shap...]
    all_to_all x2 -> x0, blocking collectives: 30.8 us -> none  [the longest x1 18.6 us: on_device(): spectra = lax.all_to_all(spectra, ('xline', 'shot'), 0, 0, tiled=True)]
    all_gather x1 -> x0, waiting for transfers between devices: 15.5 us -> none  [on_device(): running = lax.all_gather(running, 'xline', axis=0, tiled=True)]
    all_to_all x1 -> x0, starting transfers between devices: 5.38 us -> none  [on_device(): picked = lax.all_to_all(picked, ('xline', 'shot'), 0, 0, tiled=True)]
    all_to_all x1 -> x0, waiting for transfers between devices: 4.32 us -> none  [on_device(): picked = lax.all_to_all(picked, ('xline', 'shot'), 0, 0, tiled=True)]
    all_to_all x1, waiting for transfers between devices: 2.65 us -> 0.55 us  [on_device(): lax.all_to_all(jnp.broadcast_to(aperture.reshape(1, shots, gathers), (lin...]
    all_to_all x1, waiting for transfers between devices: 3.92 us -> 2.28 us  [on_device(): lax.all_to_all(traces.reshape(lines, shots * gathers, time_rows), 'xline'...]
    dot_general x1, matrix products: 1.66 us -> 0.44 us  [on_device(): jnp.einsum('skr,tsr->skt', onehot, targets, preferred_element_type=f32)]
  transfers between devices with their start and end apart: 4 -> 2, of which waited for: 4 -> 2; matrix products, arithmetic and copies ran while one was open for 6% -> 10% of each run, Pallas kernels for 0% -> 0%
where the time goes in v3:
time: 71.4 us; the launch traced here: 70.9 us
  Pallas kernels  41.3 us (58%)
  matrix products  7.95 us (11%)
  starting transfers between devices  7.64 us (11%)
  local copies, waits for them, and re-layouts  7.39 us (10%)
  other arithmetic  3.74 us (5%)
  waiting for transfers between devices  2.83 us (4%)
    pallas_call x1, Pallas kernels, on_device(): pl.pallas_call(functools.partial(spread_kernel, lines, columns), out_shap...  21.1 us
    pallas_call x1, Pallas kernels, on_device(): pl.pallas_call(functools.partial(collect_kernel, lines, columns), out_sha...  17.5 us
    all_to_all x1, starting transfers between devices, on_device(): lax.all_to_all(jnp.broadcast_to(aperture.reshape(1, shots, gathers), (lin...  4.24 us
    dot_general x1, matrix products, on_device(): jnp.einsum('tp,kt->pk', table, records.reshape(held * receivers, NT), pre...  3.68 us
    all_to_all x1, starting transfers between devices, on_device(): lax.all_to_all(traces.reshape(lines, shots * gathers, time_rows), 'xline'...  3.4 us
    pallas_call x1, Pallas kernels, on_device(): pl.pallas_call(functools.partial(mix_kernel, lines, columns, held, bins,...  2.64 us
    all_to_all x1, waiting for transfers between devices, on_device(): lax.all_to_all(traces.reshape(lines, shots * gathers, time_rows), 'xline'...  2.28 us
    convert_element_type x1, other arithmetic, fourier_table(): return table.reshape(NT, 2 * NF).astype(jnp.bfloat16)  2.1 us
  transfers between devices with their start and end apart: 2, of which 2 were waited for; matrix products, arithmetic and copies ran while one was open for 10% of the time, Pallas kernels for 0%

profile of v3, /device:TPU:0, one launch (start us, length us, event | category | flops | bytes accessed | tf_op | source)
XLA Modules:
  0.0 70.9 jit_solution(14767074257881944153)
XLA Ops:
  0.0 0.0 copy-start
  0.0 0.0 copy-start.1
  0.0 1.4 %broadcast_in_dim.49 = s32[4,4,16]{2,1,0:T(4,128)} broadcast(s32[4,16]{1,0:T(4,128)} %bitcast.55), dimensions={1,2} | broadcast | bytes 1280 | tf_op jit(solution)/shard_map/broadcast_in_dim | solution.py:253
  1.4 4.2 %all-to-all-start = ((s32[4,4,16]{2,1,0:T(4,128)}), s32[4,4,16]{2,1,0:T(4,128)S(1)}, u32[]{:S(2)}, u32[]{:S(2)}) async-start(s32[4,4,16]{2,1,0:T(4,128)} %broadcast_in_dim.49), calls=%async_computation | async-start | bytes 16384 | tf_op jit(solution)/shard_map/all_to_all | solution.py:252
  5.7 0.1 mul.144
  5.8 0.1 eq.39
  5.9 0.3 fusion.16
  6.2 0.6 select_multiply_fusion
  6.8 2.1 %add_convert_fusion = bf16[64,32,512]{2,1,0:T(8,128)(2,1)} fusion(f32[32,512]{1,0:T(8,128)S(1)} %get-tuple-element.14, f32[64,512]{1,0:T(8,128)S(1)} %get-tuple-element.13, f32[32,512]{1,0:T(8,128)S(1)} %get-tuple-element.12, f32[64,512]{1,0:T(8,128)S(1)} %get-tuple-element.11), kind=kLoop, calls=%fused_computation | loop fusion | flops 4194304 | bytes 2490368 | tf_op jit(solution)/shard_map/convert_element_type | solution.py:34
  8.9 0.6 all-to-all-done
  9.5 0.1 eq.40
  9.6 0.0 copy-done.1
  9.6 0.4 convolution_convert_fusion.2
  10.0 0.7 %copy.27 = bf16[4,4,16,512]{3,2,0,1:T(8,128)(2,1)} copy(bf16[4,4,16,512]{3,2,1,0:T(8,128)(2,1)S(1)} %bitcast.44) | data formatting | bytes 524288 | tf_op jit(solution)/shard_map/reshape | solution.py:260
  10.8 3.4 %all-to-all-start.1 = ((bf16[4,64,512]{2,1,0:T(8,128)(2,1)}), bf16[4,64,512]{2,1,0:T(8,128)(2,1)S(1)}, u32[]{:S(2)}, u32[]{:S(2)}) async-start(bf16[4,64,512]{2,1,0:T(8,128)(2,1)} %bitcast.8), calls=%async_computation.1 | async-start | bytes 524288 | tf_op jit(solution)/shard_map/all_to_all | solution.py:261
  14.2 0.0 copy-done
  14.2 3.7 %convolution_convert_fusion.1 = bf16[512,512]{1,0:T(8,128)(2,1)} fusion(bf16[2048,512]{1,0:T(8,128)(2,1)} %bitcast.40, bf16[512,2048]{1,0:T(8,128)(2,1)S(1)} %bitcast.39), kind=kOutput, calls=%fused_computation.2 | convolution fusion | flops 1074003968 | bytes 4718592 | tf_op jit(solution)/shard_map/tp,kt->pk/dot_general | solution.py:267
  17.9 2.3 %all-to-all-done.1 = bf16[4,64,512]{2,1,0:T(8,128)(2,1)S(1)} async-done(((bf16[4,64,512]{2,1,0:T(8,128)(2,1)}), bf16[4,64,512]{2,1,0:T(8,128)(2,1)S(1)}, u32[]{:S(2)}, u32[]{:S(2)}) %all-to-all-start.1) | async-done | bytes 262176 | tf_op jit(solution)/shard_map/all_to_all | solution.py:261
  20.2 2.1 %convolution_convert_fusion.3 = bf16[512,64]{0,1:T(8,128)(2,1)S(1)} fusion(bf16[64,2048]{1,0:T(8,128)(2,1)S(1)} %bitcast.45, bf16[2048,512]{1,0:T(8,128)(2,1)} %bitcast.41), kind=kOutput, calls=%fused_computation.4 | convolution fusion | flops 134250496 | bytes 2424832 | tf_op jit(solution)/shard_map/tp,kt->pk/dot_general | solution.py:265
  22.2 0.1 copy.29
  22.4 0.7 %pad_maximum_fusion.picked_ref = bf16[32,8,128]{2,1,0:T(8,128)(2,1)} fusion(bf16[32,8,64]{2,1,0:T(8,128)(2,1)S(1)} %get-tuple-element.18, bf16[32,8,64]{2,1,0:T(8,128)(2,1)S(1)} %get-tuple-element.17), kind=kLoop, calls=%fused_computation.32 | loop fusion | flops 131072 | bytes 131072 | tf_op jit(solution)/shard_map/concatenate | solution.py:273
  23.1 21.1 %shard_map.37 = (bf16[32,16,512]{2,1,0:T(8,128)(2,1)}, bf16[32,8,128]{2,1,0:T(8,128)(2,1)}) custom-call(bf16[32,16,512]{2,1,0:T(8,128)(2,1)} %bitcast.50, bf16[32,8,128]{2,1,0:T(8,128)(2,1)} %pad_maximum_fusion.picked_ref), custom_call_target="tpu_custom_call" | custom-call | tf_op jit(solution)/shard_map/pallas_call | solution.py:276
  44.2 2.6 %shard_map.38 = bf16[512,256]{1,0:T(8,128)(2,1)} custom-call(bf16[512,512]{1,0:T(8,128)(2,1)} %bitcast.52, bf16[256,128]{1,0:T(8,128)(2,1)} %bitcast.53), custom_call_target="tpu_custom_call" | custom-call | tf_op jit(solution)/shard_map/pallas_call | solution.py:288
  46.9 1.7 %copy.41 = bf16[4,2,8,8,256]{4,3,1,0,2:T(8,128)(2,1)} copy(bf16[4,2,8,8,256]{4,3,2,1,0:T(8,128)(2,1)} %bitcast.49) | data formatting | bytes 524288 | tf_op jit(solution)/shard_map/reshape | solution.py:294
  48.5 17.5 %shard_map.39 = bf16[32,4,16,256]{3,2,1,0:T(8,128)(2,1)} custom-call(bf16[8,4,16,256]{3,2,1,0:T(8,128)(2,1)} %bitcast.46), custom_call_target="tpu_custom_call" | custom-call | tf_op jit(solution)/shard_map/pallas_call | solution.py:296
  66.0 1.3 %copy.33 = bf16[32,16,4,256]{3,1,0,2:T(8,128)(2,1)S(1)} copy(bf16[32,16,4,256]{3,1,2,0:T(8,128)(2,1)} %bitcast.43) | data formatting | bytes 2097152 | tf_op jit(solution)/shard_map/transpose | solution.py:304
  67.4 1.8 %convolution_convert_fusion = bf16[512,4,256]{2,0,1:T(8,128)(2,1)S(1)} fusion(bf16[512,4,256]{2,0,1:T(8,128)(2,1)S(1)} %bitcast.47, bf16[2048,512]{1,0:T(8,128)(2,1)} %bitcast.42, s32[]{:T(128)S(6)} %select_n.31), kind=kOutput, calls=%fused_computation.1 | convolution fusion | flops 538443776 | bytes 2621444 | tf_op jit(solution)/shard_map/tp,psr->tsr/dot_general | solution.py:307
  69.1 1.8 %copy.34 = bf16[512,4,256]{2,1,0:T(4,128)(2,1)} copy(bf16[512,4,256]{2,0,1:T(8,128)(2,1)S(1)} %convolution_convert_fusion) | data formatting | bytes 2097152 | tf_op jit(solution)/shard_map/convert_element_type | solution.py:308
  (7 shorter events, 0.1 us)
Async XLA Ops:
  0.0 14.2 %copy-start = (bf16[1,2,256,2048]{3,2,1,0:T(8,128)(2,1)S(1)}, bf16[1,2,256,2048]{3,2,1,0:T(8,128)(2,1)}, u32[]{:S(2)}) copy-start(bf16[1,2,256,2048]{3,2,1,0:T(8,128)(2,1)} %param.3) | copy-start | bytes 6291460
  0.0 9.6 %copy-start.1 = (bf16[512,4,256]{2,1,0:T(4,128)(2,1)S(1)}, bf16[512,4,256]{2,1,0:T(4,128)(2,1)}, u32[]{:S(2)}) copy-start(bf16[512,4,256]{2,1,0:T(4,128)(2,1)} %param.4) | copy-start | bytes 3145732
  1.4 8.1 %all-to-all-start = ((s32[4,4,16]{2,1,0:T(4,128)}), s32[4,4,16]{2,1,0:T(4,128)S(1)}, u32[]{:S(2)}, u32[]{:S(2)}) async-start(s32[4,4,16]{2,1,0:T(4,128)} %broadcast_in_dim.49), calls=%async_computation | async-start | bytes 16384 | tf_op jit(solution)/shard_map/all_to_all | solution.py:252
  10.8 9.4 %all-to-all-start.1 = ((bf16[4,64,512]{2,1,0:T(8,128)(2,1)}), bf16[4,64,512]{2,1,0:T(8,128)(2,1)S(1)}, u32[]{:S(2)}, u32[]{:S(2)}) async-start(bf16[4,64,512]{2,1,0:T(8,128)(2,1)} %bitcast.8), calls=%async_computation.1 | async-start | bytes 524288 | tf_op jit(solution)/shard_map/all_to_all | solution.py:261

commit v4 on v3

--- a/solution.py
+++ b/solution.py
@@ -13,7 +13,7 @@
 LOW = 32
 
 
-def fourier_table(bins):
+def fourier_table(bins, start, count):
     blocks = NF // bins
     freq = jnp.arange(1, NF + 1, dtype=jnp.int32).reshape(blocks, 1, bins)
     freq = jnp.broadcast_to(freq, (blocks, 2, bins)).reshape(1, 2 * NF)
@@ -24,14 +24,14 @@
         angles = (times[:, None] * freq % NT).astype(jnp.float32) * (2.0 * math.pi / NT)
         return jnp.cos(angles), jnp.sin(angles)
 
-    cos_hi, sin_hi = trig(jnp.arange(NT // LOW, dtype=jnp.int32) * LOW)
+    cos_hi, sin_hi = trig(start + jnp.arange(count // LOW, dtype=jnp.int32) * LOW)
     cos_lo, sin_lo = trig(jnp.arange(LOW, dtype=jnp.int32))
     scale = 1.0 / math.sqrt(NT)
     first = jnp.where(is_imag, -sin_hi, cos_hi) * scale
     second = jnp.where(is_imag, -cos_hi, -sin_hi) * scale
     first, second, cos_lo, sin_lo = lax.optimization_barrier((first, second, cos_lo, sin_lo))
     table = first[:, None] * cos_lo[None] + second[:, None] * sin_lo[None]
-    return table.reshape(NT, 2 * NF).astype(jnp.bfloat16)
+    return table.reshape(count, 2 * NF).astype(jnp.bfloat16)
 
 
 def mix_kernel(lines, columns, held, bins, shots, spectra_ref, picked_ref, out_ref):
@@ -79,8 +79,15 @@
     out_ref[...] = total.astype(out_ref.dtype)
 
 
-def spread_kernel(lines, columns, spectra_ref, picked_ref, spectra_out, picked_out, send, recv, own):
+def spread_kernel(
+    lines, columns, gathers, spectra_ref, targets_ref, aperture_ref, table_ref,
+    spectra_out, picked_out,
+    apertures, traces_here, traces, picked, send, recv, own, line_send, line_recv,
+):
     devices = lines * columns
+    line = lax.axis_index("xline")
+    shots, time_rows, receivers = targets_ref.shape
+    chosen = shots * gathers
     me = lax.axis_index("xline") * columns + lax.axis_index("shot")
     mesh_id = pl.DeviceIdType.MESH
     barrier = pltpu.get_barrier_semaphore()
@@ -97,51 +104,121 @@
     lax.fori_loop(1, devices, greet, 0)
     pl.semaphore_wait(barrier, devices - 1)
 
-    def copies(step):
+    def copy_of(which, source, target, step):
         peer = lax.rem(me + step, devices)
-        return [
-            pltpu.make_async_remote_copy(
-                src_ref=source.at[peer],
-                dst_ref=target.at[me],
-                send_sem=send.at[which, step],
-                recv_sem=recv.at[which, step],
-                device_id={"xline": peer // columns, "shot": lax.rem(peer, columns)},
-                device_id_type=mesh_id,
-            )
-            for which, (source, target) in enumerate(
-                ((spectra_ref, spectra_out), (picked_ref, picked_out))
-            )
-        ]
+        return pltpu.make_async_remote_copy(
+            src_ref=source.at[peer],
+            dst_ref=target.at[me],
+            send_sem=send.at[which, step],
+            recv_sem=recv.at[which, step],
+            device_id={"xline": peer // columns, "shot": lax.rem(peer, columns)},
+            device_id_type=mesh_id,
+        )
+
+    def arrival_of(which, target, step):
+        origin = lax.rem(me + devices - step, devices)
+        return pltpu.make_async_remote_copy(
+            src_ref=target.at[origin],
+            dst_ref=target.at[origin],
+            send_sem=send.at[which, step],
+            recv_sem=recv.at[which, step],
+            device_id={"xline": origin // columns, "shot": lax.rem(origin, columns)},
+            device_id_type=mesh_id,
+        )
+
+    def along_line(which, source, target, step):
+        peer = lax.rem(line + step, lines)
+        return pltpu.make_async_remote_copy(
+            src_ref=source.at[peer] if which else source,
+            dst_ref=target.at[line],
+            send_sem=line_send.at[which, step],
+            recv_sem=line_recv.at[which, step],
+            device_id={"xline": peer},
+            device_id_type=mesh_id,
+        )
+
+    def from_line(which, target, step):
+        origin = lax.rem(line + lines - step, lines)
+        return pltpu.make_async_remote_copy(
+            src_ref=target.at[origin],
+            dst_ref=target.at[origin],
+            send_sem=line_send.at[which, step],
+            recv_sem=line_recv.at[which, step],
+            device_id={"xline": origin},
+            device_id_type=mesh_id,
+        )
 
     def begin(step, _):
-        for copy in copies(step):
-            copy.start()
-        return 0
-
-    def finish(step, _):
-        for copy in copies(step):
-            copy.wait_send()
-        origin = lax.rem(me + devices - step, devices)
-        for which, target in enumerate((spectra_out, picked_out)):
-            pltpu.make_async_remote_copy(
-                src_ref=target.at[origin],
-                dst_ref=target.at[origin],
-                send_sem=send.at[which, step],
-                recv_sem=recv.at[which, step],
-                device_id={"xline": origin // columns, "shot": lax.rem(origin, columns)},
-                device_id_type=mesh_id,
-            ).wait_recv()
-        return 0
-
-    lax.fori_loop(1, devices, begin, 0)
+        copy_of(0, spectra_ref, spectra_out, step).start()
+        return 0
+
+    for step in range(1, lines):
+        along_line(0, aperture_ref, apertures, step).start()
     mine = [
-        pltpu.make_async_copy(spectra_ref.at[me], spectra_out.at[me], own.at[0]),
-        pltpu.make_async_copy(picked_ref.at[me], picked_out.at[me], own.at[1]),
+        pltpu.make_async_copy(aperture_ref, apertures.at[line], own.at[0]),
+        pltpu.make_async_copy(spectra_ref.at[me], spectra_out.at[me], own.at[1]),
     ]
     for copy in mine:
         copy.start()
     for copy in mine:
         copy.wait()
+    for step in range(1, lines):
+        from_line(0, apertures, step).wait_recv()
+
+    wanted = jnp.concatenate([apertures[l] for l in range(lines)], axis=1)
+    lane = lax.broadcasted_iota(jnp.int32, (receivers, lines * chosen), 1)
+    receiver = lax.broadcasted_iota(jnp.int32, (receivers, lines * chosen), 0)
+    total = jnp.zeros((time_rows, lines * chosen), jnp.float32)
+    for shot in range(shots):
+        hit = (lane // gathers % shots == shot) & (receiver == wanted)
+        onehot = jnp.where(hit, 1.0, 0.0).astype(jnp.bfloat16)
+        total += jnp.dot(targets_ref[shot], onehot, preferred_element_type=jnp.float32)
+    total = total.astype(jnp.bfloat16)
+    for l in range(lines):
+        traces_here[l] = total[:, l * chosen : (l + 1) * chosen]
+
+    lax.fori_loop(1, columns, begin, 0)
+    for step in range(1, lines):
+        along_line(1, traces_here, traces, step).start()
+    lax.fori_loop(columns, devices, begin, 0)
+    keep = pltpu.make_async_copy(traces_here.at[line], traces.at[line], own.at[2])
+    keep.start()
+    keep.wait()
+    for step in range(1, lines):
+        from_line(1, traces, step).wait_recv()
+
+    value = jnp.zeros((table_ref.shape[0], chosen), jnp.float32)
+    for l in range(lines):
+        value += jnp.dot(
+            table_ref[:, l * time_rows : (l + 1) * time_rows], traces[l],
+            preferred_element_type=jnp.float32,
+        )
+    picked[...] = value.astype(jnp.bfloat16).reshape(picked.shape)
+    arrival_of(0, spectra_out, 1).wait_recv()
+
+    def begin_picked(step, _):
+        copy_of(1, picked, picked_out, step).start()
+        return 0
+
+    lax.fori_loop(1, devices, begin_picked, 0)
+    keep = pltpu.make_async_copy(picked.at[me], picked_out.at[me], own.at[3])
+    keep.start()
+    keep.wait()
+    for step in range(1, lines):
+        along_line(0, aperture_ref, apertures, step).wait_send()
+        along_line(1, traces_here, traces, step).wait_send()
+
+    def finish(step, _):
+        copy_of(0, spectra_ref, spectra_out, step).wait_send()
+        copy_of(1, picked, picked_out, step).wait_send()
+        arrival_of(1, picked_out, step).wait_recv()
+        return 0
+
+    def arrived(step, _):
+        arrival_of(0, spectra_out, step).wait_recv()
+        return 0
+
+    lax.fori_loop(2, devices, arrived, 0)
     lax.fori_loop(1, devices, finish, 0)
 
 
@@ -247,43 +324,35 @@
     time_rows, shots, receivers = targets.shape
     held = records.shape[1]
     gathers = aperture.shape[2]
-    table = fourier_table(bins)
-
-    apertures = lax.all_to_all(
-        jnp.broadcast_to(aperture.reshape(1, shots, gathers), (lines, shots, gathers)),
-        "xline", 0, 0, tiled=True,
-    )
-    receiver_ids = jnp.arange(receivers, dtype=jnp.int32)
-    chosen = apertures.transpose(1, 0, 2).reshape(shots, lines * gathers)
-    onehot = (chosen[:, :, None] == receiver_ids).astype(bf16)
-    traces = jnp.einsum("skr,tsr->skt", onehot, targets, preferred_element_type=f32).astype(bf16)
-    traces = traces.reshape(shots, lines, gathers, time_rows).transpose(1, 0, 2, 3)
-    traces = lax.all_to_all(
-        traces.reshape(lines, shots * gathers, time_rows), "xline", 0, 0, tiled=True
-    )
-    traces = traces.transpose(1, 0, 2).reshape(shots * gathers, NT)
-    picked = jnp.einsum("tp,kt->pk", table, traces, preferred_element_type=f32).astype(bf16)
+    table = fourier_table(bins, 0, NT).T
+    chosen = shots * gathers
 
     spectra = jnp.einsum(
-        "tp,kt->pk", table, records.reshape(held * receivers, NT), preferred_element_type=f32
+        "pt,kt->pk", table, records.reshape(held * receivers, NT), preferred_element_type=f32
     ).astype(bf16)
 
     spectra = spectra.reshape(devices, 2 * bins, held * receivers)
-    picked = picked.reshape(devices, 2, bins, shots * gathers)
-    picked = jnp.concatenate([picked[:, 0], picked[:, 1]], axis=-1)
     in_vmem = pl.BlockSpec(memory_space=pltpu.VMEM)
     dma = pltpu.SemaphoreType.DMA
     spectra, picked = pl.pallas_call(
-        functools.partial(spread_kernel, lines, columns),
+        functools.partial(spread_kernel, lines, columns, gathers),
         out_shape=[
             jax.ShapeDtypeStruct(spectra.shape, bf16),
-            jax.ShapeDtypeStruct(picked.shape, bf16),
+            jax.ShapeDtypeStruct((devices, 2 * bins, chosen), bf16),
         ],
-        in_specs=[in_vmem] * 2,
+        in_specs=[in_vmem] * 4,
         out_specs=[in_vmem] * 2,
-        scratch_shapes=[dma((2, devices)), dma((2, devices)), dma((2,))],
+        scratch_shapes=[
+            pltpu.VMEM((lines, 1, chosen), jnp.int32),
+            pltpu.VMEM((lines, time_rows, chosen), bf16),
+            pltpu.VMEM((lines, time_rows, chosen), bf16),
+            pltpu.VMEM((devices, 2 * bins, chosen), bf16),
+            dma((2, devices)), dma((2, devices)), dma((4,)), dma((2, lines)), dma((2, lines)),
+        ],
         compiler_params=pltpu.CompilerParams(collective_id=0, has_side_effects=True),
-    )(spectra, picked)
+    )(spectra, targets.transpose(1, 0, 2), aperture.reshape(1, chosen), table)
+    picked = picked.reshape(devices, 2, bins, chosen)
+    picked = jnp.concatenate([picked[:, 0], picked[:, 1]], axis=-1)
 
     running = pl.pallas_call(
         functools.partial(mix_kernel, lines, columns, held, bins, shots),
@@ -303,7 +372,7 @@
     )(running)
     running = running.transpose(0, 2, 1, 3).reshape(2 * NF, shots, receivers)
 
-    rows = lax.dynamic_slice_in_dim(table, lax.axis_index("xline") * time_rows, time_rows, 0)
+    rows = fourier_table(bins, lax.axis_index("xline") * time_rows, time_rows)
     out = jnp.einsum("tp,psr->tsr", rows * 2, running, preferred_element_type=f32)
     return out.astype(bf16)
 

time: 71.4 us -> 72.1 us (level)
  Pallas kernels: 41.3 us -> 50.4 us
  starting transfers between devices: 7.64 us -> 0 us
  local copies, waits for them, and re-layouts: 7.39 us -> 12 us
  matrix products: 7.95 us -> 4.49 us
  waiting for transfers between devices: 2.83 us -> 0 us
  other arithmetic: 3.74 us -> 4.65 us
    pallas_call x1, Pallas kernels: 21.1 us -> 30 us  [on_device(): pl.pallas_call(functools.partial(spread_kernel, lines, columns, gathers),...]
    all_to_all x2 -> x0, starting transfers between devices: 7.64 us -> none  [the longest x1 4.24 us: on_device(): lax.all_to_all(jnp.broadcast_to(aperture.reshape(1, shots, gathers), (lin...]
    convert_element_type x1, local copies, waits for them, and re-layouts: 0.12 us -> 3.99 us  [fourier_table(): return table.reshape(count, 2 * NF).astype(jnp.bfloat16)]
    all_to_all x2 -> x0, waiting for transfers between devices: 2.83 us -> none  [the longest x1 2.28 us: on_device(): lax.all_to_all(traces.reshape(lines, shots * gathers, time_rows), 'xline'...]
    dot_general x3 -> x1, matrix products: 6.19 us -> 3.78 us  [on_device(): jnp.einsum('pt,kt->pk', table, records.reshape(held * receivers, NT), pre...]
    unnamed x4 -> x8, local copies, waits for them, and re-layouts: 0.01 us -> 1.63 us
    broadcast_in_dim x1 -> x0, local copies, waits for them, and re-layouts: 1.44 us -> none  [on_device(): jnp.broadcast_to(aperture.reshape(1, shots, gathers), (lines, shots, gath...]
    dot_general x1, matrix products: 1.76 us -> 0.71 us  [on_device(): jnp.einsum('tp,psr->tsr', rows * 2, running, preferred_element_type=f32)]
  transfers between devices with their start and end apart: 2 -> 0, of which waited for: 2 -> 0; matrix products, arithmetic and copies ran while one was open for 10% -> 0% of each run, Pallas kernels for 0% -> 0%
where the time goes in v4:
time: 72.1 us; the launch traced here: 71.7 us
  Pallas kernels  50.4 us (70%)
  local copies, waits for them, and re-layouts  12 us (17%)
  other arithmetic  4.65 us (6%)
  matrix products  4.49 us (6%)
    pallas_call x1, Pallas kernels, on_device(): pl.pallas_call(functools.partial(spread_kernel, lines, columns, gathers),...  30 us
    pallas_call x1, Pallas kernels, on_device(): pl.pallas_call(functools.partial(collect_kernel, lines, columns), out_sha...  17.8 us
    convert_element_type x1, local copies, waits for them, and re-layouts, fourier_table(): return table.reshape(count, 2 * NF).astype(jnp.bfloat16)  3.99 us
    dot_general x1, matrix products, on_device(): jnp.einsum('pt,kt->pk', table, records.reshape(held * receivers, NT), pre...  3.78 us
    pallas_call x1, Pallas kernels, on_device(): pl.pallas_call(functools.partial(mix_kernel, lines, columns, held, bins,...  2.64 us
    convert_element_type x1, other arithmetic, fourier_table(): return table.reshape(count, 2 * NF).astype(jnp.bfloat16)  2.06 us
    convert_element_type x1, local copies, waits for them, and re-layouts, on_device(): return out.astype(bf16)  1.78 us
    reshape x1, local copies, waits for them, and re-layouts, on_device(): running.reshape(shots, 2, columns, bins, receivers).transpose(2, 0, 1, 3, 4)  1.66 us

profile of v4, /device:TPU:0, one launch (start us, length us, event | category | flops | bytes accessed | tf_op | source)
XLA Modules:
  0.0 71.7 jit_solution(9550332161653736413)
XLA Ops:
  0.0 0.0 copy-start
  0.0 0.1 mul.246
  0.2 0.1 eq.32
  0.3 0.6 select_multiply_fusion
  0.9 0.3 fusion.14
  1.2 2.1 %add_convert_fusion = bf16[64,32,512]{2,1,0:T(8,128)(2,1)} fusion(f32[32,512]{1,0:T(8,128)S(1)} %get-tuple-element.22, f32[64,512]{1,0:T(8,128)S(1)} %get-tuple-element.21, f32[32,512]{1,0:T(8,128)S(1)} %get-tuple-element.20, f32[64,512]{1,0:T(8,128)S(1)} %get-tuple-element.19), kind=kLoop, calls=%fused_computation | loop fusion | flops 4194304 | bytes 2490368 | tf_op jit(solution)/shard_map/convert_element_type | solution.py:34
  3.2 4.0 %copy.12 = bf16[2048,512]{0,1:T(8,128)(2,1)} copy(bf16[2048,512]{1,0:T(8,128)(2,1)} %bitcast.34) | data formatting | bytes 4194304 | tf_op jit(solution)/shard_map/convert_element_type | solution.py:34
  7.2 0.0 copy-done
  7.2 0.0 copy-start.1
  7.2 3.8 %convolution_convert_fusion.1 = bf16[512,512]{1,0:T(8,128)(2,1)} fusion(bf16[2048,512]{1,0:T(8,128)(2,1)} %bitcast.35, bf16[512,2048]{1,0:T(8,128)(2,1)S(1)} %bitcast.32), kind=kOutput, calls=%fused_computation.2 | convolution fusion | flops 1074003968 | bytes 4718592 | tf_op jit(solution)/shard_map/pt,kt->pk/dot_general | solution.py:330
  11.0 0.0 copy-start.2
  11.0 0.0 copy-done.1
  11.0 1.1 %copy.22 = bf16[512,4,256]{2,0,1:T(8,128)(2,1)} copy(bf16[512,4,256]{2,1,0:T(4,128)(2,1)S(1)} %copy-done.1) | data formatting | bytes 2097152 | tf_op args[1]
  12.1 0.5 broadcast.168
  12.6 0.0 copy-done.2
  12.6 0.6 reduce.3
  13.2 0.6 reshape.120.aperture_ref
  13.8 30.0 %shard_map.37 = (bf16[32,16,512]{2,1,0:T(8,128)(2,1)}, bf16[32,16,64]{2,1,0:T(8,128)(2,1)}) custom-call(bf16[32,16,512]{2,1,0:T(8,128)(2,1)} %bitcast.43, bf16[4,512,256]{2,1,0:T(8,128)(2,1)} %bitcast.37, s32[1,64]{1,0:T(1,128)} %reshape.120.aperture_ref, bf16[512,2048]{1,0:T(8,128)(2,1)} %bitcast.33), custom_call_target="tpu_custom_call" | custom-call | tf_op jit(solution)/shard_map/pallas_call | solution.py:337
  43.8 0.9 %slice_bitcast_fusion.1 = (bf16[256,64]{1,0:T(8,128)(2,1)S(1)}, bf16[256,64]{1,0:T(8,128)(2,1)S(1)}) fusion(bf16[32,2,8,64]{3,2,1,0:T(8,128)(2,1)} %bitcast.44), kind=kLoop, calls=%fused_computation.25 | loop fusion | bytes 131072 | tf_op jit(solution)/shard_map/concatenate | solution.py:355
  44.6 0.7 pad_maximum_fusion.picked_ref
  45.4 2.6 %shard_map.38 = bf16[512,256]{1,0:T(8,128)(2,1)} custom-call(bf16[512,512]{1,0:T(8,128)(2,1)} %bitcast.42, bf16[256,128]{1,0:T(8,128)(2,1)} %pad_maximum_fusion.picked_ref), custom_call_target="tpu_custom_call" | custom-call | tf_op jit(solution)/shard_map/pallas_call | solution.py:357
  48.0 1.7 %copy.23 = bf16[4,2,8,8,256]{4,3,1,0,2:T(8,128)(2,1)} copy(bf16[4,2,8,8,256]{4,3,2,1,0:T(8,128)(2,1)} %bitcast.40) | data formatting | bytes 524288 | tf_op jit(solution)/shard_map/reshape | solution.py:363
  49.7 17.8 %shard_map.39 = bf16[32,4,16,256]{3,2,1,0:T(8,128)(2,1)} custom-call(bf16[8,4,16,256]{3,2,1,0:T(8,128)(2,1)} %bitcast.38), custom_call_target="tpu_custom_call" | custom-call | tf_op jit(solution)/shard_map/pallas_call | solution.py:365
  67.5 1.3 %copy.16 = bf16[32,16,4,256]{3,1,0,2:T(8,128)(2,1)S(1)} copy(bf16[32,16,4,256]{3,1,2,0:T(8,128)(2,1)} %bitcast.36) | data formatting | bytes 2097152 | tf_op jit(solution)/shard_map/transpose | solution.py:373
  68.8 0.2 select_multiply_fusion.2
  69.0 0.2 fusion
  69.2 0.7 convolution_convert_fusion
  69.9 1.8 %copy.17 = bf16[512,4,256]{2,1,0:T(4,128)(2,1)} copy(bf16[512,4,256]{2,0,1:T(8,128)(2,1)S(1)} %convolution_convert_fusion) | data formatting | bytes 2097152 | tf_op jit(solution)/shard_map/convert_element_type | solution.py:377
  (5 shorter events, 0.0 us)
Async XLA Ops:
  0.0 7.2 %copy-start = (bf16[1,2,256,2048]{3,2,1,0:T(8,128)(2,1)S(1)}, bf16[1,2,256,2048]{3,2,1,0:T(8,128)(2,1)}, u32[]{:S(2)}) copy-start(bf16[1,2,256,2048]{3,2,1,0:T(8,128)(2,1)} %param.3) | copy-start | bytes 6291460
  7.2 3.8 %copy-start.1 = (bf16[512,4,256]{2,1,0:T(4,128)(2,1)S(1)}, bf16[512,4,256]{2,1,0:T(4,128)(2,1)}, u32[]{:S(2)}) copy-start(bf16[512,4,256]{2,1,0:T(4,128)(2,1)} %param.4) | copy-start | bytes 3145732
  11.0 1.6 %copy-start.2 = (s32[4,1,16]{2,1,0:T(1,128)S(1)}, s32[4,1,16]{2,1,0:T(1,128)}, u32[]{:S(2)}) copy-start(s32[4,1,16]{2,1,0:T(1,128)} %param.5) | copy-start | bytes 772

commit v5 on v4

--- a/solution.py
+++ b/solution.py
@@ -32,6 +32,39 @@
     first, second, cos_lo, sin_lo = lax.optimization_barrier((first, second, cos_lo, sin_lo))
     table = first[:, None] * cos_lo[None] + second[:, None] * sin_lo[None]
     return table.reshape(count, 2 * NF).astype(jnp.bfloat16)
+
+
+def table_kernel(first_ref, second_ref, cos_ref, sin_ref, out_ref):
+    low = cos_ref.shape[1]
+    for hi in range(first_ref.shape[1]):
+        out_ref[:, hi * low : (hi + 1) * low] = (
+            first_ref[:, hi : hi + 1] * cos_ref[...] + second_ref[:, hi : hi + 1] * sin_ref[...]
+        ).astype(out_ref.dtype)
+
+
+def transposed_table(bins):
+    low, blocks = 128, NF // bins
+    freq = jnp.arange(1, NF + 1, dtype=jnp.int32).reshape(blocks, 1, bins)
+    freq = jnp.broadcast_to(freq, (blocks, 2, bins)).reshape(2 * NF, 1)
+    is_imag = jnp.arange(2, dtype=jnp.int32).reshape(1, 2, 1)
+    is_imag = jnp.broadcast_to(is_imag, (blocks, 2, bins)).reshape(2 * NF, 1) == 1
+
+    def trig(times):
+        angles = (freq * times[None, :] % NT).astype(jnp.float32) * (2.0 * math.pi / NT)
+        return jnp.cos(angles), jnp.sin(angles)
+
+    cos_hi, sin_hi = trig(jnp.arange(NT // low, dtype=jnp.int32) * low)
+    cos_lo, sin_lo = trig(jnp.arange(low, dtype=jnp.int32))
+    scale = 1.0 / math.sqrt(NT)
+    first = jnp.where(is_imag, -sin_hi, cos_hi) * scale
+    second = jnp.where(is_imag, -cos_hi, -sin_hi) * scale
+    in_vmem = pl.BlockSpec(memory_space=pltpu.VMEM)
+    return pl.pallas_call(
+        table_kernel,
+        out_shape=jax.ShapeDtypeStruct((2 * NF, NT), jnp.bfloat16),
+        in_specs=[in_vmem] * 4,
+        out_specs=in_vmem,
+    )(first, second, cos_lo, sin_lo)
 
 
 def mix_kernel(lines, columns, held, bins, shots, spectra_ref, picked_ref, out_ref):
@@ -86,6 +119,7 @@
 ):
     devices = lines * columns
     line = lax.axis_index("xline")
+    shot_here = lax.axis_index("shot")
     shots, time_rows, receivers = targets_ref.shape
     chosen = shots * gathers
     me = lax.axis_index("xline") * columns + lax.axis_index("shot")
@@ -104,8 +138,13 @@
     lax.fori_loop(1, devices, greet, 0)
     pl.semaphore_wait(barrier, devices - 1)
 
+    def line_of(step):
+        far, other = step // columns // 2, lax.rem(step // columns, 2)
+        moved = lax.rem(line + far * (lines // 2), lines)
+        return moved + other * (1 - 2 * lax.rem(moved, 2))
+
     def copy_of(which, source, target, step):
-        peer = lax.rem(me + step, devices)
+        peer = line_of(step) * columns + lax.rem(shot_here + step, columns)
         return pltpu.make_async_remote_copy(
             src_ref=source.at[peer],
             dst_ref=target.at[me],
@@ -116,7 +155,7 @@
         )
 
     def arrival_of(which, target, step):
-        origin = lax.rem(me + devices - step, devices)
+        origin = line_of(step) * columns + lax.rem(shot_here + devices - step, columns)
         return pltpu.make_async_remote_copy(
             src_ref=target.at[origin],
             dst_ref=target.at[origin],
@@ -154,6 +193,7 @@
 
     for step in range(1, lines):
         along_line(0, aperture_ref, apertures, step).start()
+    lax.fori_loop(1, 2 * columns, begin, 0)
     mine = [
         pltpu.make_async_copy(aperture_ref, apertures.at[line], own.at[0]),
         pltpu.make_async_copy(spectra_ref.at[me], spectra_out.at[me], own.at[1]),
@@ -165,7 +205,9 @@
     for step in range(1, lines):
         from_line(0, apertures, step).wait_recv()
 
-    wanted = jnp.concatenate([apertures[l] for l in range(lines)], axis=1)
+    wanted = jnp.concatenate(
+        [apertures[l, s : s + 1, :] for l in range(lines) for s in range(shots)], axis=1
+    )
     lane = lax.broadcasted_iota(jnp.int32, (receivers, lines * chosen), 1)
     receiver = lax.broadcasted_iota(jnp.int32, (receivers, lines * chosen), 0)
     total = jnp.zeros((time_rows, lines * chosen), jnp.float32)
@@ -177,10 +219,10 @@
     for l in range(lines):
         traces_here[l] = total[:, l * chosen : (l + 1) * chosen]
 
-    lax.fori_loop(1, columns, begin, 0)
+    arrival_of(0, spectra_out, 1).wait_recv()
     for step in range(1, lines):
         along_line(1, traces_here, traces, step).start()
-    lax.fori_loop(columns, devices, begin, 0)
+    lax.fori_loop(2 * columns, devices, begin, 0)
     keep = pltpu.make_async_copy(traces_here.at[line], traces.at[line], own.at[2])
     keep.start()
     keep.wait()
@@ -194,7 +236,7 @@
             preferred_element_type=jnp.float32,
         )
     picked[...] = value.astype(jnp.bfloat16).reshape(picked.shape)
-    arrival_of(0, spectra_out, 1).wait_recv()
+    arrival_of(0, spectra_out, 2).wait_recv()
 
     def begin_picked(step, _):
         copy_of(1, picked, picked_out, step).start()
@@ -218,7 +260,7 @@
         arrival_of(0, spectra_out, step).wait_recv()
         return 0
 
-    lax.fori_loop(2, devices, arrived, 0)
+    lax.fori_loop(3, devices, arrived, 0)
     lax.fori_loop(1, devices, finish, 0)
 
 
@@ -324,7 +366,7 @@
     time_rows, shots, receivers = targets.shape
     held = records.shape[1]
     gathers = aperture.shape[2]
-    table = fourier_table(bins, 0, NT).T
+    table = transposed_table(bins)
     chosen = shots * gathers
 
     spectra = jnp.einsum(
@@ -343,14 +385,14 @@
         in_specs=[in_vmem] * 4,
         out_specs=[in_vmem] * 2,
         scratch_shapes=[
-            pltpu.VMEM((lines, 1, chosen), jnp.int32),
+            pltpu.VMEM((lines, shots, gathers), jnp.int32),
             pltpu.VMEM((lines, time_rows, chosen), bf16),
             pltpu.VMEM((lines, time_rows, chosen), bf16),
             pltpu.VMEM((devices, 2 * bins, chosen), bf16),
             dma((2, devices)), dma((2, devices)), dma((4,)), dma((2, lines)), dma((2, lines)),
         ],
         compiler_params=pltpu.CompilerParams(collective_id=0, has_side_effects=True),
-    )(spectra, targets.transpose(1, 0, 2), aperture.reshape(1, chosen), table)
+    )(spectra, targets.transpose(1, 0, 2), aperture.reshape(shots, gathers), table)
     picked = picked.reshape(devices, 2, bins, chosen)
     picked = jnp.concatenate([picked[:, 0], picked[:, 1]], axis=-1)
 

time: 72.1 us -> 72.7 us (level)
  local copies, waits for them, and re-layouts: 12 us -> 6.98 us
  Pallas kernels: 50.4 us -> 55.4 us
  other arithmetic: 4.65 us -> 5.42 us
    pallas_call x0 -> x1, Pallas kernels: none -> 4.78 us  [transposed_table(): pl.pallas_call(table_kernel, out_shape=jax.ShapeDtypeStruct((2 * NF, NT),...]
    convert_element_type x1 -> x0, local copies, waits for them, and re-layouts: 3.99 us -> none  [fourier_table(): return table.reshape(count, 2 * NF).astype(jnp.bfloat16)]
    mul x1 -> x2, other arithmetic: 0.01 us -> 2.12 us  [the longest x1 2.11 us: transposed_table(): second = jnp.where(is_imag, -cos_hi, -sin_hi) * scale]
    convert_element_type x1 -> x0, other arithmetic: 2.06 us -> none  [fourier_table(): return table.reshape(count, 2 * NF).astype(jnp.bfloat16)]
    sin x1 -> x2, other arithmetic: 0.27 us -> 2.19 us  [trig(): return (jnp.cos(angles), jnp.sin(angles))]
    pallas_call x1, Pallas kernels: 30 us -> 31.2 us  [on_device(): pl.pallas_call(functools.partial(spread_kernel, lines, columns, gathers),...]
    pallas_call x1, Pallas kernels: 17.8 us -> 16.7 us  [on_device(): pl.pallas_call(functools.partial(collect_kernel, lines, columns), out_sha...]
    unnamed x8 -> x5, local copies, waits for them, and re-layouts: 1.63 us -> 1.12 us
where the time goes in v5:
time: 72.7 us; the launch traced here: 72.4 us
  Pallas kernels  55.4 us (76%)
  local copies, waits for them, and re-layouts  6.98 us (10%)
  other arithmetic  5.42 us (7%)
  matrix products  4.48 us (6%)
    pallas_call x1, Pallas kernels, on_device(): pl.pallas_call(functools.partial(spread_kernel, lines, columns, gathers),...  31.2 us
    pallas_call x1, Pallas kernels, on_device(): pl.pallas_call(functools.partial(collect_kernel, lines, columns), out_sha...  16.7 us
    pallas_call x1, Pallas kernels, transposed_table(): pl.pallas_call(table_kernel, out_shape=jax.ShapeDtypeStruct((2 * NF, NT),...  4.78 us
    dot_general x1, matrix products, on_device(): jnp.einsum('pt,kt->pk', table, records.reshape(held * receivers, NT), pre...  3.77 us
    pallas_call x1, Pallas kernels, on_device(): pl.pallas_call(functools.partial(mix_kernel, lines, columns, held, bins,...  2.64 us
    sin x2, other arithmetic, trig(): return (jnp.cos(angles), jnp.sin(angles))  2.19 us
    mul x1, other arithmetic, transposed_table(): second = jnp.where(is_imag, -cos_hi, -sin_hi) * scale  2.11 us
    convert_element_type x1, local copies, waits for them, and re-layouts, on_device(): return out.astype(bf16)  1.78 us

profile of v5, /device:TPU:0, one launch (start us, length us, event | category | flops | bytes accessed | tf_op | source)
XLA Modules:
  0.0 72.4 jit_solution(5541511004152193808)
XLA Ops:
  0.0 0.0 copy-start
  0.0 0.1 mul.205
  0.2 0.1 eq.43
  0.3 2.1 %select_multiply_fusion = (f32[512,16]{1,0:T(8,128)}, f32[512,16]{1,0:T(8,128)}) fusion(s32[16]{0:T(128)S(1)} %iota_multiply_fusion, s32[512]{0:T(512)S(1)} %mul.205, pred[512]{0:T(512)(128)(4,1)S(1)} %eq.43), kind=kLoop, calls=%fused_computation.22 | loop fusion | flops 163840 | bytes 68160 | tf_op jit(solution)/shard_map/mul | solution.py:60
  2.4 1.9 %fusion.10 = (f32[512,128]{1,0:T(8,128)}, f32[512,128]{1,0:T(8,128)}) fusion(s32[512]{0:T(512)S(1)} %mul.205), kind=kLoop, calls=%fused_computation.26 | loop fusion | flops 917504 | bytes 526336 | tf_op jit(solution)/shard_map/sin | solution.py:54
  4.3 4.8 %shard_map.37.table_ref = bf16[512,2048]{1,0:T(8,128)(2,1)} custom-call(f32[512,16]{1,0:T(8,128)} %get-tuple-element.20.first_ref, f32[512,16]{1,0:T(8,128)} %get-tuple-element.19.second_ref, f32[512,128]{1,0:T(8,128)} %get-tuple-element.24.cos_ref, f32[512,128]{1,0:T(8,128)} %get-tuple-element.23.sin_ref), custom_call_target="tpu_custom_call" | custom-call | tf_op jit(solution)/shard_map/pallas_call | solution.py:62
  9.1 0.0 copy-done
  9.1 0.0 copy-start.1
  9.1 3.8 %convolution_convert_fusion.1 = bf16[512,512]{1,0:T(8,128)(2,1)} fusion(bf16[512,2048]{1,0:T(8,128)(2,1)} %shard_map.37.table_ref, bf16[512,2048]{1,0:T(8,128)(2,1)S(1)} %bitcast.31), kind=kOutput, calls=%fused_computation.1 | convolution fusion | flops 1074003968 | bytes 4718592 | tf_op jit(solution)/shard_map/pt,kt->pk/dot_general | solution.py:372
  12.8 0.0 copy-done.1
  12.9 1.1 %copy.19 = bf16[512,4,256]{2,0,1:T(8,128)(2,1)} copy(bf16[512,4,256]{2,1,0:T(4,128)(2,1)S(1)} %copy-done.1) | data formatting | bytes 2097152 | tf_op args[1]
  14.0 31.2 %shard_map.38 = (bf16[32,16,512]{2,1,0:T(8,128)(2,1)}, bf16[32,16,64]{2,1,0:T(8,128)(2,1)}) custom-call(bf16[32,16,512]{2,1,0:T(8,128)(2,1)} %bitcast.37, bf16[4,512,256]{2,1,0:T(8,128)(2,1)} %bitcast.32, s32[4,16]{1,0:T(4,128)} %bitcast.41, bf16[512,2048]{1,0:T(8,128)(2,1)} %shard_map.37.table_ref), custom_call_target="tpu_custom_call" | custom-call | tf_op jit(solution)/shard_map/pallas_call | solution.py:379
  45.2 0.9 %slice_bitcast_fusion.1 = (bf16[256,64]{1,0:T(8,128)(2,1)S(1)}, bf16[256,64]{1,0:T(8,128)(2,1)S(1)}) fusion(bf16[32,2,8,64]{3,2,1,0:T(8,128)(2,1)} %bitcast.40), kind=kLoop, calls=%fused_computation.36 | loop fusion | bytes 131072 | tf_op jit(solution)/shard_map/concatenate | solution.py:397
  46.1 0.7 pad_maximum_fusion.picked_ref
  46.8 2.6 %shard_map.39 = bf16[512,256]{1,0:T(8,128)(2,1)} custom-call(bf16[512,512]{1,0:T(8,128)(2,1)} %bitcast.39, bf16[256,128]{1,0:T(8,128)(2,1)} %pad_maximum_fusion.picked_ref), custom_call_target="tpu_custom_call" | custom-call | tf_op jit(solution)/shard_map/pallas_call | solution.py:399
  49.4 1.7 %copy.20 = bf16[4,2,8,8,256]{4,3,1,0,2:T(8,128)(2,1)} copy(bf16[4,2,8,8,256]{4,3,2,1,0:T(8,128)(2,1)} %bitcast.36) | data formatting | bytes 524288 | tf_op jit(solution)/shard_map/reshape | solution.py:405
  51.1 16.7 %shard_map.40 = bf16[32,4,16,256]{3,2,1,0:T(8,128)(2,1)} custom-call(bf16[8,4,16,256]{3,2,1,0:T(8,128)(2,1)} %bitcast.34), custom_call_target="tpu_custom_call" | custom-call | tf_op jit(solution)/shard_map/pallas_call | solution.py:407
  67.9 1.3 %copy.13 = bf16[32,16,4,256]{3,1,0,2:T(8,128)(2,1)S(1)} copy(bf16[32,16,4,256]{3,1,2,0:T(8,128)(2,1)} %bitcast.33) | data formatting | bytes 2097152 | tf_op jit(solution)/shard_map/transpose | solution.py:415
  69.2 0.2 select_multiply_fusion.2
  69.4 0.3 fusion.22
  69.7 0.2 fusion
  69.9 0.7 convolution_convert_fusion
  70.6 1.8 %copy.14 = bf16[512,4,256]{2,1,0:T(4,128)(2,1)} copy(bf16[512,4,256]{2,0,1:T(8,128)(2,1)S(1)} %convolution_convert_fusion) | data formatting | bytes 2097152 | tf_op jit(solution)/shard_map/convert_element_type | solution.py:419
  (5 shorter events, 0.0 us)
Async XLA Ops:
  0.0 9.1 %copy-start = (bf16[1,2,256,2048]{3,2,1,0:T(8,128)(2,1)S(1)}, bf16[1,2,256,2048]{3,2,1,0:T(8,128)(2,1)}, u32[]{:S(2)}) copy-start(bf16[1,2,256,2048]{3,2,1,0:T(8,128)(2,1)} %param.3) | copy-start | bytes 6291460
  9.1 3.8 %copy-start.1 = (bf16[512,4,256]{2,1,0:T(4,128)(2,1)S(1)}, bf16[512,4,256]{2,1,0:T(4,128)(2,1)}, u32[]{:S(2)}) copy-start(bf16[512,4,256]{2,1,0:T(4,128)(2,1)} %param.4) | copy-start | bytes 3145732

commit v6 on v4

--- a/solution.py
+++ b/solution.py
@@ -86,8 +86,9 @@
 ):
     devices = lines * columns
     line = lax.axis_index("xline")
+    shot_here = lax.axis_index("shot")
     shots, time_rows, receivers = targets_ref.shape
-    chosen = shots * gathers
+    width = traces.shape[2]
     me = lax.axis_index("xline") * columns + lax.axis_index("shot")
     mesh_id = pl.DeviceIdType.MESH
     barrier = pltpu.get_barrier_semaphore()
@@ -104,8 +105,13 @@
     lax.fori_loop(1, devices, greet, 0)
     pl.semaphore_wait(barrier, devices - 1)
 
+    def line_of(step):
+        far, other = step // columns // 2, lax.rem(step // columns, 2)
+        moved = lax.rem(line + far * (lines // 2), lines)
+        return moved + other * (1 - 2 * lax.rem(moved, 2))
+
     def copy_of(which, source, target, step):
-        peer = lax.rem(me + step, devices)
+        peer = line_of(step) * columns + lax.rem(shot_here + step, columns)
         return pltpu.make_async_remote_copy(
             src_ref=source.at[peer],
             dst_ref=target.at[me],
@@ -116,7 +122,7 @@
         )
 
     def arrival_of(which, target, step):
-        origin = lax.rem(me + devices - step, devices)
+        origin = line_of(step) * columns + lax.rem(shot_here + devices - step, columns)
         return pltpu.make_async_remote_copy(
             src_ref=target.at[origin],
             dst_ref=target.at[origin],
@@ -154,6 +160,7 @@
 
     for step in range(1, lines):
         along_line(0, aperture_ref, apertures, step).start()
+    lax.fori_loop(1, 2 * columns, begin, 0)
     mine = [
         pltpu.make_async_copy(aperture_ref, apertures.at[line], own.at[0]),
         pltpu.make_async_copy(spectra_ref.at[me], spectra_out.at[me], own.at[1]),
@@ -165,36 +172,41 @@
     for step in range(1, lines):
         from_line(0, apertures, step).wait_recv()
 
-    wanted = jnp.concatenate([apertures[l] for l in range(lines)], axis=1)
-    lane = lax.broadcasted_iota(jnp.int32, (receivers, lines * chosen), 1)
-    receiver = lax.broadcasted_iota(jnp.int32, (receivers, lines * chosen), 0)
-    total = jnp.zeros((time_rows, lines * chosen), jnp.float32)
+    wanted = []
+    for l in range(lines):
+        wanted += [apertures[l, s : s + 1, :] for s in range(shots)]
+        if width > shots * gathers:
+            wanted.append(jnp.zeros((1, width - shots * gathers), jnp.int32))
+    wanted = jnp.concatenate(wanted, axis=1)
+    lane = lax.broadcasted_iota(jnp.int32, (receivers, lines * width), 1)
+    receiver = lax.broadcasted_iota(jnp.int32, (receivers, lines * width), 0)
+    total = jnp.zeros((time_rows, lines * width), jnp.float32)
     for shot in range(shots):
-        hit = (lane // gathers % shots == shot) & (receiver == wanted)
+        hit = (lane % width // gathers == shot) & (receiver == wanted)
         onehot = jnp.where(hit, 1.0, 0.0).astype(jnp.bfloat16)
         total += jnp.dot(targets_ref[shot], onehot, preferred_element_type=jnp.float32)
     total = total.astype(jnp.bfloat16)
     for l in range(lines):
-        traces_here[l] = total[:, l * chosen : (l + 1) * chosen]
-
-    lax.fori_loop(1, columns, begin, 0)
+        traces_here[l] = total[:, l * width : (l + 1) * width]
+
+    arrival_of(0, spectra_out, 1).wait_recv()
     for step in range(1, lines):
         along_line(1, traces_here, traces, step).start()
-    lax.fori_loop(columns, devices, begin, 0)
+    lax.fori_loop(2 * columns, devices, begin, 0)
     keep = pltpu.make_async_copy(traces_here.at[line], traces.at[line], own.at[2])
     keep.start()
     keep.wait()
     for step in range(1, lines):
         from_line(1, traces, step).wait_recv()
 
-    value = jnp.zeros((table_ref.shape[0], chosen), jnp.float32)
+    value = jnp.zeros((table_ref.shape[0], width), jnp.float32)
     for l in range(lines):
         value += jnp.dot(
             table_ref[:, l * time_rows : (l + 1) * time_rows], traces[l],
             preferred_element_type=jnp.float32,
         )
     picked[...] = value.astype(jnp.bfloat16).reshape(picked.shape)
-    arrival_of(0, spectra_out, 1).wait_recv()
+    arrival_of(0, spectra_out, 2).wait_recv()
 
     def begin_picked(step, _):
         copy_of(1, picked, picked_out, step).start()
@@ -218,7 +230,7 @@
         arrival_of(0, spectra_out, step).wait_recv()
         return 0
 
-    lax.fori_loop(2, devices, arrived, 0)
+    lax.fori_loop(3, devices, arrived, 0)
     lax.fori_loop(1, devices, finish, 0)
 
 
@@ -326,6 +338,7 @@
     gathers = aperture.shape[2]
     table = fourier_table(bins, 0, NT).T
     chosen = shots * gathers
+    padded = -(-chosen // 128) * 128
 
     spectra = jnp.einsum(
         "pt,kt->pk", table, records.reshape(held * receivers, NT), preferred_element_type=f32
@@ -338,20 +351,20 @@
         functools.partial(spread_kernel, lines, columns, gathers),
         out_shape=[
             jax.ShapeDtypeStruct(spectra.shape, bf16),
-            jax.ShapeDtypeStruct((devices, 2 * bins, chosen), bf16),
+            jax.ShapeDtypeStruct((devices, 2 * bins, padded), bf16),
         ],
         in_specs=[in_vmem] * 4,
         out_specs=[in_vmem] * 2,
         scratch_shapes=[
-            pltpu.VMEM((lines, 1, chosen), jnp.int32),
-            pltpu.VMEM((lines, time_rows, chosen), bf16),
-            pltpu.VMEM((lines, time_rows, chosen), bf16),
-            pltpu.VMEM((devices, 2 * bins, chosen), bf16),
+            pltpu.VMEM((lines, shots, gathers), jnp.int32),
+            pltpu.VMEM((lines, time_rows, padded), bf16),
+            pltpu.VMEM((lines, time_rows, padded), bf16),
+            pltpu.VMEM((devices, 2 * bins, padded), bf16),
             dma((2, devices)), dma((2, devices)), dma((4,)), dma((2, lines)), dma((2, lines)),
         ],
         compiler_params=pltpu.CompilerParams(collective_id=0, has_side_effects=True),
-    )(spectra, targets.transpose(1, 0, 2), aperture.reshape(1, chosen), table)
-    picked = picked.reshape(devices, 2, bins, chosen)
+    )(spectra, targets.transpose(1, 0, 2), aperture.reshape(shots, gathers), table)
+    picked = picked.reshape(devices, 2, bins, padded)[..., :chosen]
     picked = jnp.concatenate([picked[:, 0], picked[:, 1]], axis=-1)
 
     running = pl.pallas_call(

time: 72.1 us -> 71.3 us (0.989)
  local copies, waits for them, and re-layouts: 12 us -> 10.9 us
  Pallas kernels: 50.4 us -> 51.4 us
    pallas_call x1, Pallas kernels: 30 us -> 31.8 us  [on_device(): pl.pallas_call(functools.partial(spread_kernel, lines, columns, gathers),...]
    pallas_call x1, Pallas kernels: 17.8 us -> 16.9 us  [on_device(): pl.pallas_call(functools.partial(collect_kernel, lines, columns), out_sha...]
    unnamed x8 -> x5, local copies, waits for them, and re-layouts: 1.63 us -> 1.12 us
where the time goes in v6:
time: 71.3 us; the launch traced here: 71 us
  Pallas kernels  51.4 us (72%)
  local copies, waits for them, and re-layouts  10.9 us (15%)
  matrix products  4.49 us (6%)
  other arithmetic  4.1 us (6%)
    pallas_call x1, Pallas kernels, on_device(): pl.pallas_call(functools.partial(spread_kernel, lines, columns, gathers),...  31.8 us
    pallas_call x1, Pallas kernels, on_device(): pl.pallas_call(functools.partial(collect_kernel, lines, columns), out_sha...  16.9 us
    convert_element_type x1, local copies, waits for them, and re-layouts, fourier_table(): return table.reshape(count, 2 * NF).astype(jnp.bfloat16)  3.95 us
    dot_general x1, matrix products, on_device(): jnp.einsum('pt,kt->pk', table, records.reshape(held * receivers, NT), pre...  3.78 us
    pallas_call x1, Pallas kernels, on_device(): pl.pallas_call(functools.partial(mix_kernel, lines, columns, held, bins,...  2.64 us
    convert_element_type x1, other arithmetic, fourier_table(): return table.reshape(count, 2 * NF).astype(jnp.bfloat16)  2.07 us
    convert_element_type x1, local copies, waits for them, and re-layouts, on_device(): return out.astype(bf16)  1.78 us
    reshape x1, local copies, waits for them, and re-layouts, on_device(): running.reshape(shots, 2, columns, bins, receivers).transpose(2, 0, 1, 3, 4)  1.68 us

profile of v6, /device:TPU:0, one launch (start us, length us, event | category | flops | bytes accessed | tf_op | source)
XLA Modules:
  0.0 71.0 jit_solution(1567367934647537296)
XLA Ops:
  0.0 0.0 copy-start
  0.0 0.1 mul.246
  0.2 0.1 eq.32
  0.3 0.6 select_multiply_fusion
  0.9 0.3 fusion.14
  1.2 2.1 %add_convert_fusion = bf16[64,32,512]{2,1,0:T(8,128)(2,1)} fusion(f32[32,512]{1,0:T(8,128)S(1)} %get-tuple-element.22, f32[64,512]{1,0:T(8,128)S(1)} %get-tuple-element.21, f32[32,512]{1,0:T(8,128)S(1)} %get-tuple-element.20, f32[64,512]{1,0:T(8,128)S(1)} %get-tuple-element.19), kind=kLoop, calls=%fused_computation | loop fusion | flops 4194304 | bytes 2490368 | tf_op jit(solution)/shard_map/convert_element_type | solution.py:34
  3.2 3.9 %copy.12 = bf16[2048,512]{0,1:T(8,128)(2,1)} copy(bf16[2048,512]{1,0:T(8,128)(2,1)} %bitcast.35) | data formatting | bytes 4194304 | tf_op jit(solution)/shard_map/convert_element_type | solution.py:34
  7.2 0.0 copy-done
  7.2 0.0 copy-start.1
  7.2 3.8 %convolution_convert_fusion.1 = bf16[512,512]{1,0:T(8,128)(2,1)} fusion(bf16[2048,512]{1,0:T(8,128)(2,1)} %bitcast.36, bf16[512,2048]{1,0:T(8,128)(2,1)S(1)} %bitcast.33), kind=kOutput, calls=%fused_computation.2 | convolution fusion | flops 1074003968 | bytes 4718592 | tf_op jit(solution)/shard_map/pt,kt->pk/dot_general | solution.py:343
  11.0 0.0 copy-done.1
  11.0 1.1 %copy.22 = bf16[512,4,256]{2,0,1:T(8,128)(2,1)} copy(bf16[512,4,256]{2,1,0:T(4,128)(2,1)S(1)} %copy-done.1) | data formatting | bytes 2097152 | tf_op args[1]
  12.1 31.8 %shard_map.37 = (bf16[32,16,512]{2,1,0:T(8,128)(2,1)}, bf16[32,16,128]{2,1,0:T(8,128)(2,1)}) custom-call(bf16[32,16,512]{2,1,0:T(8,128)(2,1)} %bitcast.42, bf16[4,512,256]{2,1,0:T(8,128)(2,1)} %bitcast.37, s32[4,16]{1,0:T(4,128)} %bitcast.46, bf16[512,2048]{1,0:T(8,128)(2,1)} %bitcast.34), custom_call_target="tpu_custom_call" | custom-call | tf_op jit(solution)/shard_map/pallas_call | solution.py:350
  43.9 0.9 %slice_bitcast_fusion.1 = (bf16[256,64]{1,0:T(8,128)(2,1)S(1)}, bf16[256,64]{1,0:T(8,128)(2,1)S(1)}) fusion(bf16[32,2,8,128]{3,2,1,0:T(8,128)(2,1)} %bitcast.45), kind=kLoop, calls=%fused_computation.25 | loop fusion | bytes 131072 | tf_op jit(solution)/shard_map/concatenate | solution.py:368
  44.8 0.7 %pad_maximum_fusion.picked_ref = bf16[256,128]{1,0:T(8,128)(2,1)} fusion(bf16[256,64]{1,0:T(8,128)(2,1)S(1)} %get-tuple-element.26, bf16[256,64]{1,0:T(8,128)(2,1)S(1)} %get-tuple-element.25), kind=kLoop, calls=%fused_computation.26 | loop fusion | flops 131072 | bytes 131072 | tf_op jit(solution)/shard_map/concatenate | solution.py:368
  45.5 2.6 %shard_map.38 = bf16[512,256]{1,0:T(8,128)(2,1)} custom-call(bf16[512,512]{1,0:T(8,128)(2,1)} %bitcast.44, bf16[256,128]{1,0:T(8,128)(2,1)} %pad_maximum_fusion.picked_ref), custom_call_target="tpu_custom_call" | custom-call | tf_op jit(solution)/shard_map/pallas_call | solution.py:370
  48.2 1.7 %copy.23 = bf16[4,2,8,8,256]{4,3,1,0,2:T(8,128)(2,1)} copy(bf16[4,2,8,8,256]{4,3,2,1,0:T(8,128)(2,1)} %bitcast.41) | data formatting | bytes 524288 | tf_op jit(solution)/shard_map/reshape | solution.py:376
  49.9 16.9 %shard_map.39 = bf16[32,4,16,256]{3,2,1,0:T(8,128)(2,1)} custom-call(bf16[8,4,16,256]{3,2,1,0:T(8,128)(2,1)} %bitcast.39), custom_call_target="tpu_custom_call" | custom-call | tf_op jit(solution)/shard_map/pallas_call | solution.py:378
  66.7 1.3 %copy.16 = bf16[32,16,4,256]{3,1,0,2:T(8,128)(2,1)S(1)} copy(bf16[32,16,4,256]{3,1,2,0:T(8,128)(2,1)} %bitcast.38) | data formatting | bytes 2097152 | tf_op jit(solution)/shard_map/transpose | solution.py:386
  68.1 0.2 select_multiply_fusion.2
  68.3 0.2 fusion
  68.5 0.7 %convolution_convert_fusion = bf16[512,4,256]{2,0,1:T(8,128)(2,1)S(1)} fusion(bf16[512,512,1]{1,0,2:T(8,128)(2,1)S(1)} %bitcast.43, bf16[512,4,256]{2,0,1:T(8,128)(2,1)S(1)} %bitcast.40), kind=kOutput, calls=%fused_computation.1 | convolution fusion | flops 537395200 | bytes 2621440 | tf_op jit(solution)/shard_map/tp,psr->tsr/dot_general | solution.py:389
  69.2 1.8 %copy.17 = bf16[512,4,256]{2,1,0:T(4,128)(2,1)} copy(bf16[512,4,256]{2,0,1:T(8,128)(2,1)S(1)} %convolution_convert_fusion) | data formatting | bytes 2097152 | tf_op jit(solution)/shard_map/convert_element_type | solution.py:390
  (5 shorter events, 0.0 us)
Async XLA Ops:
  0.0 7.2 %copy-start = (bf16[1,2,256,2048]{3,2,1,0:T(8,128)(2,1)S(1)}, bf16[1,2,256,2048]{3,2,1,0:T(8,128)(2,1)}, u32[]{:S(2)}) copy-start(bf16[1,2,256,2048]{3,2,1,0:T(8,128)(2,1)} %param.3) | copy-start | bytes 6291460
  7.2 3.8 %copy-start.1 = (bf16[512,4,256]{2,1,0:T(4,128)(2,1)S(1)}, bf16[512,4,256]{2,1,0:T(4,128)(2,1)}, u32[]{:S(2)}) copy-start(bf16[512,4,256]{2,1,0:T(4,128)(2,1)} %param.4) | copy-start | bytes 3145732

commit v7 on v6

--- a/solution.py
+++ b/solution.py
@@ -199,10 +199,11 @@
     for step in range(1, lines):
         from_line(1, traces, step).wait_recv()
 
-    value = jnp.zeros((table_ref.shape[0], width), jnp.float32)
+    value = jnp.zeros((table_ref.shape[1], width), jnp.float32)
     for l in range(lines):
-        value += jnp.dot(
-            table_ref[:, l * time_rows : (l + 1) * time_rows], traces[l],
+        value += lax.dot_general(
+            table_ref[l * time_rows : (l + 1) * time_rows, :], traces[l],
+            (((0,), (0,)), ((), ())),
             preferred_element_type=jnp.float32,
         )
     picked[...] = value.astype(jnp.bfloat16).reshape(picked.shape)
@@ -336,12 +337,12 @@
     time_rows, shots, receivers = targets.shape
     held = records.shape[1]
     gathers = aperture.shape[2]
-    table = fourier_table(bins, 0, NT).T
+    table = fourier_table(bins, 0, NT)
     chosen = shots * gathers
     padded = -(-chosen // 128) * 128
 
     spectra = jnp.einsum(
-        "pt,kt->pk", table, records.reshape(held * receivers, NT), preferred_element_type=f32
+        "tp,kt->pk", table, records.reshape(held * receivers, NT), preferred_element_type=f32
     ).astype(bf16)
 
     spectra = spectra.reshape(devices, 2 * bins, held * receivers)

time: 71.3 us -> 64.3 us (0.902)
  local copies, waits for them, and re-layouts: 10.9 us -> 6.99 us
  matrix products: 4.49 us -> 2.82 us
  other arithmetic: 4.1 us -> 2.75 us
    convert_element_type x1 -> x0, local copies, waits for them, and re-layouts: 3.95 us -> none  [fourier_table(): return table.reshape(count, 2 * NF).astype(jnp.bfloat16)]
    dot_general x1, matrix products: 3.78 us -> 2.1 us  [on_device(): jnp.einsum('tp,kt->pk', table, records.reshape(held * receivers, NT), pre...]
    convert_element_type x1, other arithmetic: 2.07 us -> 0.73 us  [fourier_table(): return table.reshape(count, 2 * NF).astype(jnp.bfloat16)]
where the time goes in v7:
time: 64.3 us; the launch traced here: 64 us
  Pallas kernels  51.4 us (80%)
  local copies, waits for them, and re-layouts  6.99 us (11%)
  matrix products  2.82 us (4%)
  other arithmetic  2.75 us (4%)
    pallas_call x1, Pallas kernels, on_device(): pl.pallas_call(functools.partial(spread_kernel, lines, columns, gathers),...  31.8 us
    pallas_call x1, Pallas kernels, on_device(): pl.pallas_call(functools.partial(collect_kernel, lines, columns), out_sha...  16.9 us
    pallas_call x1, Pallas kernels, on_device(): pl.pallas_call(functools.partial(mix_kernel, lines, columns, held, bins,...  2.64 us
    dot_general x1, matrix products, on_device(): jnp.einsum('tp,kt->pk', table, records.reshape(held * receivers, NT), pre...  2.1 us
    convert_element_type x1, local copies, waits for them, and re-layouts, on_device(): return out.astype(bf16)  1.78 us
    reshape x1, local copies, waits for them, and re-layouts, on_device(): running.reshape(shots, 2, columns, bins, receivers).transpose(2, 0, 1, 3, 4)  1.67 us
    transpose x1, local copies, waits for them, and re-layouts, on_device(): running = running.transpose(0, 2, 1, 3).reshape(2 * NF, shots, receivers)  1.31 us

profile of v7, /device:TPU:0, one launch (start us, length us, event | category | flops | bytes accessed | tf_op | source)
XLA Modules:
  0.0 64.0 jit_solution(961525669321689826)
XLA Ops:
  0.0 0.0 copy-start
  0.0 0.1 mul.246
  0.2 0.1 eq.32
  0.3 0.6 select_multiply_fusion
  0.9 0.3 fusion.14
  1.2 0.7 %add_convert_fusion = bf16[64,32,512]{2,1,0:T(8,128)(2,1)S(1)} fusion(f32[32,512]{1,0:T(8,128)S(1)} %get-tuple-element.22, f32[64,512]{1,0:T(8,128)S(1)} %get-tuple-element.21, f32[32,512]{1,0:T(8,128)S(1)} %get-tuple-element.20, f32[64,512]{1,0:T(8,128)S(1)} %get-tuple-element.19), kind=kLoop, calls=%fused_computation | loop fusion | flops 4194304 | bytes 2490368 | tf_op jit(solution)/shard_map/convert_element_type | solution.py:34
  1.9 0.0 copy-start.1
  1.9 0.0 copy-done
  1.9 0.0 copy-start.2
  1.9 2.1 %convolution_convert_fusion.1 = bf16[512,512]{1,0:T(8,128)(2,1)} fusion(bf16[2048,512]{1,0:T(8,128)(2,1)S(1)} %bitcast.33, bf16[512,2048]{1,0:T(8,128)(2,1)S(1)} %bitcast.32), kind=kOutput, calls=%fused_computation.2 | convolution fusion | flops 1074003968 | bytes 4718592 | tf_op jit(solution)/shard_map/tp,kt->pk/dot_general | solution.py:344
  4.0 0.0 copy-done.1
  4.0 0.0 copy-done.2
  4.0 1.1 %copy.19 = bf16[512,4,256]{2,0,1:T(8,128)(2,1)} copy(bf16[512,4,256]{2,1,0:T(4,128)(2,1)S(1)} %copy-done.2) | data formatting | bytes 2097152 | tf_op args[1]
  5.2 31.8 %shard_map.37 = (bf16[32,16,512]{2,1,0:T(8,128)(2,1)}, bf16[32,16,128]{2,1,0:T(8,128)(2,1)}) custom-call(bf16[32,16,512]{2,1,0:T(8,128)(2,1)} %bitcast.40, bf16[4,512,256]{2,1,0:T(8,128)(2,1)} %bitcast.35, s32[4,16]{1,0:T(4,128)} %bitcast.44, bf16[2048,512]{1,0:T(8,128)(2,1)} %bitcast.34), custom_call_target="tpu_custom_call" | custom-call | tf_op jit(solution)/shard_map/pallas_call | solution.py:351
  37.0 0.9 %slice_bitcast_fusion.1 = (bf16[256,64]{1,0:T(8,128)(2,1)S(1)}, bf16[256,64]{1,0:T(8,128)(2,1)S(1)}) fusion(bf16[32,2,8,128]{3,2,1,0:T(8,128)(2,1)} %bitcast.43), kind=kLoop, calls=%fused_computation.25 | loop fusion | bytes 131072 | tf_op jit(solution)/shard_map/concatenate | solution.py:369
  37.9 0.7 %pad_maximum_fusion.picked_ref = bf16[256,128]{1,0:T(8,128)(2,1)} fusion(bf16[256,64]{1,0:T(8,128)(2,1)S(1)} %get-tuple-element.26, bf16[256,64]{1,0:T(8,128)(2,1)S(1)} %get-tuple-element.25), kind=kLoop, calls=%fused_computation.26 | loop fusion | flops 131072 | bytes 131072 | tf_op jit(solution)/shard_map/concatenate | solution.py:369
  38.6 2.6 %shard_map.38 = bf16[512,256]{1,0:T(8,128)(2,1)} custom-call(bf16[512,512]{1,0:T(8,128)(2,1)} %bitcast.42, bf16[256,128]{1,0:T(8,128)(2,1)} %pad_maximum_fusion.picked_ref), custom_call_target="tpu_custom_call" | custom-call | tf_op jit(solution)/shard_map/pallas_call | solution.py:371
  41.3 1.7 %copy.20 = bf16[4,2,8,8,256]{4,3,1,0,2:T(8,128)(2,1)} copy(bf16[4,2,8,8,256]{4,3,2,1,0:T(8,128)(2,1)} %bitcast.39) | data formatting | bytes 524288 | tf_op jit(solution)/shard_map/reshape | solution.py:377
  42.9 16.9 %shard_map.39 = bf16[32,4,16,256]{3,2,1,0:T(8,128)(2,1)} custom-call(bf16[8,4,16,256]{3,2,1,0:T(8,128)(2,1)} %bitcast.37), custom_call_target="tpu_custom_call" | custom-call | tf_op jit(solution)/shard_map/pallas_call | solution.py:379
  59.8 1.3 %copy.13 = bf16[32,16,4,256]{3,1,0,2:T(8,128)(2,1)S(1)} copy(bf16[32,16,4,256]{3,1,2,0:T(8,128)(2,1)} %bitcast.36) | data formatting | bytes 2097152 | tf_op jit(solution)/shard_map/transpose | solution.py:387
  61.1 0.2 select_multiply_fusion.2
  61.4 0.2 fusion
  61.5 0.7 %convolution_convert_fusion = bf16[512,4,256]{2,0,1:T(8,128)(2,1)S(1)} fusion(bf16[512,512,1]{1,0,2:T(8,128)(2,1)S(1)} %bitcast.41, bf16[512,4,256]{2,0,1:T(8,128)(2,1)S(1)} %bitcast.38), kind=kOutput, calls=%fused_computation.1 | convolution fusion | flops 537395200 | bytes 2621440 | tf_op jit(solution)/shard_map/tp,psr->tsr/dot_general | solution.py:390
  62.3 1.8 %copy.14 = bf16[512,4,256]{2,1,0:T(4,128)(2,1)} copy(bf16[512,4,256]{2,0,1:T(8,128)(2,1)S(1)} %convolution_convert_fusion) | data formatting | bytes 2097152 | tf_op jit(solution)/shard_map/convert_element_type | solution.py:391
  (5 shorter events, 0.0 us)
Async XLA Ops:
  0.0 1.9 %copy-start = (bf16[1,2,256,2048]{3,2,1,0:T(8,128)(2,1)S(1)}, bf16[1,2,256,2048]{3,2,1,0:T(8,128)(2,1)}, u32[]{:S(2)}) copy-start(bf16[1,2,256,2048]{3,2,1,0:T(8,128)(2,1)} %param.3) | copy-start | bytes 6291460
  1.9 2.1 %copy-start.1 = (bf16[64,32,512]{2,1,0:T(8,128)(2,1)}, bf16[64,32,512]{2,1,0:T(8,128)(2,1)S(1)}, u32[]{:S(2)}) copy-start(bf16[64,32,512]{2,1,0:T(8,128)(2,1)S(1)} %add_convert_fusion) | copy-start | bytes 6291460
  1.9 2.1 %copy-start.2 = (bf16[512,4,256]{2,1,0:T(4,128)(2,1)S(1)}, bf16[512,4,256]{2,1,0:T(4,128)(2,1)}, u32[]{:S(2)}) copy-start(bf16[512,4,256]{2,1,0:T(4,128)(2,1)} %param.4) | copy-start | bytes 3145732
